TPU v7x, 32 devices: a whole 2x2x4 slice. The times are simulated.
32 devices in a mesh: dp: 16 (over z, y, x), tensor: 2 (over core).
Axes of the slice: x: 2, y: 2, z: 4, core: 2. Of those that a mesh axis runs over, the one named last changes fastest.
Arguments:
- block_in: bfloat16 [32768, 1536], P('dp'), may hold values from -30 to 30
- prefix_len: int32 [32], P('dp'), may hold values from 0 to 1024
- out_grad: bfloat16 [32768, 1536], P('dp'), may hold values from -6 to 6
- step_count: int32 [1], replicated, may hold values from 2 to 20
- q_weight: float32 [1536, 1536], P('dp', 'tensor'), may hold values from -0.15625 to 0.15625
- key_matrix: float32 [1536, 768], P('dp', 'tensor'), may hold values from -0.15625 to 0.15625
- value_matrix: float32 [1536, 768], P('dp', 'tensor'), may hold values from -0.15625 to 0.15625
- o_weight: float32 [1536, 1536], P('dp', 'tensor'), may hold values from -2.5 to 2.5
- gate_weight: float32 [1536, 4096], P('dp', 'tensor'), may hold values from -0.15625 to 0.15625
- up_weight: float32 [1536, 4096], P('dp', 'tensor'), may hold values from -0.15625 to 0.15625
- down_weight: float32 [1536, 4096], P('dp', 'tensor'), may hold values from -0.1875 to 0.1875
- norm_gains: float32 [2, 1536], replicated, may hold values from 0.25 to 1.75
- query_mean_moment: float32 [1536, 1536], P('dp', 'tensor'), may hold values from -0.00018310547 to 0.00018310547
- key_mean_moment: float32 [1536, 768], P('dp', 'tensor'), may hold values from -0.00024414062 to 0.00024414062
- value_mean_moment: float32 [1536, 768], P('dp', 'tensor'), may hold values from -0.00024414062 to 0.00024414062
- output_mean_moment: float32 [1536, 1536], P('dp', 'tensor'), may hold values from -1.335144e-05 to 1.335144e-05
- gate_mean_moment: float32 [1536, 4096], P('dp', 'tensor'), may hold values from -9.1552734e-05 to 9.1552734e-05
- up_mean_moment: float32 [1536, 4096], P('dp', 'tensor'), may hold values from -0.00010681152 to 0.00010681152
- down_mean_moment: float32 [1536, 4096], P('dp', 'tensor'), may hold values from -7.6293945e-05 to 7.6293945e-05
- gains_mean_moment: float32 [2, 1536], P(None, 'dp'), may hold values from -0.00024414062 to 0.00024414062
- q_second: float32 [1536, 1536], P('dp', 'tensor'), may hold values from 4.571947e-09 to 1.8287787e-08
- key_square_moment: float32 [1536, 768], P('dp', 'tensor'), may hold values from 9.321445e-09 to 3.7374555e-08
- value_square_moment: float32 [1536, 768], P('dp', 'tensor'), may hold values from 9.321445e-09 to 3.7374555e-08
- o_second: float32 [1536, 1536], P('dp', 'tensor'), may hold values from 2.3525551e-11 to 9.321445e-11
- gate_second: float32 [1536, 4096], P('dp', 'tensor'), may hold values from 1.0519916e-09 to 4.2035277e-09
- up_second: float32 [1536, 4096], P('dp', 'tensor'), may hold values from 1.2384205e-09 to 4.953682e-09
- down_second: float32 [1536, 4096], P('dp', 'tensor'), may hold values from 8.3893004e-10 to 3.3645977e-09
- gains_second: float32 [2, 1536], P(None, 'dp'), may hold values from 7.102053e-09 to 4.4387832e-08
Outputs:
- block_out: bfloat16 [32768, 1536], P('dp')
- in_grad: float32 [32768, 1536], P('dp')
- grad_norm: float32 [1], replicated
- new_q_weight: float32 [1536, 1536], P('dp', 'tensor')
- new_k_weight: float32 [1536, 768], P('dp', 'tensor')
- new_v_weight: float32 [1536, 768], P('dp', 'tensor')
- new_o_weight: float32 [1536, 1536], P('dp', 'tensor')
- new_gate_weight: float32 [1536, 4096], P('dp', 'tensor')
- new_up_weight: float32 [1536, 4096], P('dp', 'tensor')
- new_down_weight: float32 [1536, 4096], P('dp', 'tensor')
- new_norm_gains: float32 [2, 1536], P(None, 'dp')
- new_q_first: float32 [1536, 1536], P('dp', 'tensor')
- new_k_first: float32 [1536, 768], P('dp', 'tensor')
- new_v_first: float32 [1536, 768], P('dp', 'tensor')
- new_o_first: float32 [1536, 1536], P('dp', 'tensor')
- new_gate_first: float32 [1536, 4096], P('dp', 'tensor')
- new_up_first: float32 [1536, 4096], P('dp', 'tensor')
- new_down_first: float32 [1536, 4096], P('dp', 'tensor')
- new_gains_first: float32 [2, 1536], P(None, 'dp')
- new_q_second: float32 [1536, 1536], P('dp', 'tensor')
- new_k_second: float32 [1536, 768], P('dp', 'tensor')
- new_v_second: float32 [1536, 768], P('dp', 'tensor')
- new_o_second: float32 [1536, 1536], P('dp', 'tensor')
- new_gate_second: float32 [1536, 4096], P('dp', 'tensor')
- new_up_second: float32 [1536, 4096], P('dp', 'tensor')
- new_down_second: float32 [1536, 4096], P('dp', 'tensor')
- new_gains_second: float32 [2, 1536], P(None, 'dp')
All inputs are finite; a program needn't handle non-finite values.
Results may differ from a plain program's by a relative error of at most 0.018.
Values may be sent and summed in bfloat16 or wider, within the bound.
A program may use at most 320 MiB of HBM per device.

v0:
```python
import math

import jax
import jax.numpy as jnp
from jax import lax
from jax.sharding import PartitionSpec as P

QUERY_HEADS = 16
KEY_VALUE_HEADS = 8
HEAD_WIDTH = 96
SEQUENCE_LENGTH = 1024
MICRO = 2
SEQ_MB = 1
QUERY_BLOCK_ROWS = 512


theta_base = 100000.0
norm_eps = 1e-05
beta_one = 0.9
beta_two = 0.95
adam_eps = 1e-08
decay_rate = 0.1
clip_limit = 1.0
neg_fill = -1e30
matrix_rates = (0.08, 0.08, 0.08, 1.0, 0.08, 0.08, 0.1)
gain_rate = 1.0


def rotary_tables(length, head_size):
    half_size = head_size // 2
    frequency = jnp.power(theta_base, -2.0 * jnp.arange(half_size, dtype=jnp.float32) / head_size)
    angles = jnp.arange(length, dtype=jnp.float32)[:, None] * frequency[None, :]
    cosine_values = jnp.cos(angles)
    sine_values = jnp.sin(angles)
    return (
        jnp.concatenate([cosine_values, cosine_values], 1)[:, None, :],
        jnp.concatenate([sine_values, sine_values], 1)[:, None, :],
    )


def rotary_apply(values, cosine_values, sine_values):
    half_size = values.shape[-1] // 2
    turned = jnp.concatenate([-values[..., half_size:], values[..., :half_size]], -1)
    return values * cosine_values + turned * sine_values


def unrotate(gradient, cosine_values, sine_values):
    half_size = gradient.shape[-1] // 2
    spun_grad = gradient * sine_values
    turned = jnp.concatenate([spun_grad[..., half_size:], -spun_grad[..., :half_size]], -1)
    return gradient * cosine_values + turned


def normalize(row_values):
    inverse = lax.rsqrt(jnp.mean(row_values * row_values, -1, keepdims=True) + norm_eps)
    return (row_values * inverse, inverse)


def norm_back(dnorm, gain_row, unit_rows, inverse):
    scaled = dnorm * gain_row
    return inverse * (scaled - unit_rows * jnp.mean(scaled * unit_rows, -1, keepdims=True))


def contract_rows(left_side, right_side):
    return lax.dot_general(
        left_side, right_side, (((0,), (0,)), ((), ())), preferred_element_type=jnp.float32
    )


def times_transpose(left_side, right_side):
    return lax.dot_general(
        left_side, right_side, (((1,), (1,)), ((), ())), preferred_element_type=jnp.float32
    )


def masked_scores(q_block, key_row_slice, first_row, prefix, key_count):
    score_scale = 1.0 / math.sqrt(HEAD_WIDTH)
    raw_scores = (
        jnp.einsum("qhgd,khd->hgqk", q_block, key_row_slice, preferred_element_type=jnp.float32)
        * score_scale
    )
    query_places = first_row + lax.broadcasted_iota(jnp.int32, (q_block.shape[0], key_count), 0)
    key_places = lax.broadcasted_iota(jnp.int32, (q_block.shape[0], key_count), 1)
    return jnp.where((key_places <= query_places) | (key_places < prefix), raw_scores, neg_fill)


def forward_block(q_block, key_row_slice, value_row_slice, first_row, prefix, key_count):
    scores = masked_scores(q_block, key_row_slice, first_row, prefix, key_count)
    row_peak = jnp.max(scores, -1, keepdims=True)
    exponent = jnp.exp(scores - row_peak)
    row_total = jnp.sum(exponent, -1, keepdims=True)
    probability = (exponent / row_total).astype(jnp.bfloat16)
    mixed_out = jnp.einsum(
        "hgqk,khd->qhgd", probability, value_row_slice, preferred_element_type=jnp.float32
    )
    return (mixed_out, row_peak[..., 0] + jnp.log(row_total[..., 0]))


def backward_block(
    q_block, key_row_slice, value_row_slice, dmixed, logsum, first_row, prefix, key_count
):
    score_scale = 1.0 / math.sqrt(HEAD_WIDTH)
    scores = masked_scores(q_block, key_row_slice, first_row, prefix, key_count)
    probability = jnp.exp(scores - logsum[..., None])
    dprobs = jnp.einsum(
        "qhgd,khd->hgqk", dmixed, value_row_slice, preferred_element_type=jnp.float32
    )
    dscores = (probability * (dprobs - jnp.sum(probability * dprobs, -1, keepdims=True))).astype(
        jnp.bfloat16
    )
    dquery = (
        jnp.einsum("hgqk,khd->qhgd", dscores, key_row_slice, preferred_element_type=jnp.float32)
        * score_scale
    )
    d_key = (
        jnp.einsum("hgqk,qhgd->khd", dscores, q_block, preferred_element_type=jnp.float32)
        * score_scale
    )
    dvalue = jnp.einsum(
        "hgqk,qhgd->khd",
        probability.astype(jnp.bfloat16),
        dmixed,
        preferred_element_type=jnp.float32,
    )
    return (dquery, d_key, dvalue)


def run_block(block_fn, block_index, prefix, operands):
    first_row = block_index * QUERY_BLOCK_ROWS
    result = block_fn(*operands, first_row, prefix, SEQUENCE_LENGTH)
    return result


def attend_forward(q_seq, key_row_slice, value_row_slice, prefix):
    block_list = SEQUENCE_LENGTH // QUERY_BLOCK_ROWS

    def one_block(block_index):
        q_block = lax.dynamic_slice_in_dim(
            q_seq, block_index * QUERY_BLOCK_ROWS, QUERY_BLOCK_ROWS, 0
        )
        return run_block(
            forward_block, block_index, prefix, (q_block, key_row_slice, value_row_slice)
        )

    return lax.map(one_block, jnp.arange(block_list, dtype=jnp.int32))


def attend_backward(q_seq, key_row_slice, value_row_slice, dmixed_seq, logsums, prefix):
    block_list = SEQUENCE_LENGTH // QUERY_BLOCK_ROWS

    def one_block(running, scan_item):
        block_index, logsum = scan_item
        q_block = lax.dynamic_slice_in_dim(
            q_seq, block_index * QUERY_BLOCK_ROWS, QUERY_BLOCK_ROWS, 0
        )
        d_block = lax.dynamic_slice_in_dim(
            dmixed_seq, block_index * QUERY_BLOCK_ROWS, QUERY_BLOCK_ROWS, 0
        )
        dquery, d_key, dvalue = run_block(
            backward_block,
            block_index,
            prefix,
            (q_block, key_row_slice, value_row_slice, d_block, logsum),
        )
        return ((running[0] + d_key, running[1] + dvalue), dquery)

    zero_keys = jnp.zeros(key_row_slice.shape, jnp.float32)
    (dkeys, dvalues), dqueries = lax.scan(
        one_block, (zero_keys, zero_keys), (jnp.arange(block_list, dtype=jnp.int32), logsums)
    )
    return (dqueries.reshape(SEQUENCE_LENGTH, -1, HEAD_WIDTH), dkeys, dvalues)


def run_micro(input_low, back_rows, prefixes, weights, norm_gains, cosine_values, sine_values):
    q_full, k_full, v_full, o_full, gate_full, up_full, down_full = weights
    row_count = input_low.shape[0]
    sequence_count = row_count // SEQUENCE_LENGTH
    q_heads = q_full.shape[1] // HEAD_WIDTH
    kv_heads = k_full.shape[1] // HEAD_WIDTH
    group_width = QUERY_HEADS // KEY_VALUE_HEADS
    input_rows = input_low.astype(jnp.float32)
    unit_one, inverse_one = normalize(input_rows)
    first_normed_input = (unit_one * norm_gains[0]).astype(jnp.bfloat16)
    query_raw = jnp.dot(first_normed_input, q_full, preferred_element_type=jnp.float32)
    key_raw = jnp.dot(first_normed_input, k_full, preferred_element_type=jnp.float32)
    value_low = jnp.dot(first_normed_input, v_full, preferred_element_type=jnp.float32).astype(
        jnp.bfloat16
    )
    query_turned = rotary_apply(
        query_raw.reshape(sequence_count, SEQUENCE_LENGTH, q_heads, HEAD_WIDTH),
        cosine_values,
        sine_values,
    ).astype(jnp.bfloat16)
    key_turned = rotary_apply(
        key_raw.reshape(sequence_count, SEQUENCE_LENGTH, kv_heads, HEAD_WIDTH),
        cosine_values,
        sine_values,
    ).astype(jnp.bfloat16)
    query_grouped = query_turned.reshape(
        sequence_count, SEQUENCE_LENGTH, kv_heads, group_width, HEAD_WIDTH
    )
    value_seqs = value_low.reshape(sequence_count, SEQUENCE_LENGTH, kv_heads, HEAD_WIDTH)
    seq_index = 0
    mixed_out, logsums = attend_forward(
        query_grouped[seq_index], key_turned[seq_index], value_seqs[seq_index], prefixes[seq_index]
    )
    mixed_list = mixed_out.reshape(SEQUENCE_LENGTH, q_heads * HEAD_WIDTH)
    logsum_list = [logsums]
    mixed_low = mixed_list.astype(jnp.bfloat16)
    attn_out = lax.psum(times_transpose(mixed_low, o_full).astype(jnp.bfloat16), "tensor").astype(
        jnp.float32
    )
    middle = input_rows + attn_out
    unit_two, inverse_two = normalize(middle)
    normed_two = (unit_two * norm_gains[1]).astype(jnp.bfloat16)
    gate_value = jnp.dot(normed_two, gate_full, preferred_element_type=jnp.float32)
    up_value = jnp.dot(normed_two, up_full, preferred_element_type=jnp.float32)
    gate_sigmoid = jax.nn.sigmoid(gate_value)
    gated_value = gate_value * gate_sigmoid
    hidden = (gated_value * up_value).astype(jnp.bfloat16)
    ffn_out = lax.psum(times_transpose(hidden, down_full).astype(jnp.bfloat16), "tensor").astype(
        jnp.float32
    )
    block_out = (middle + ffn_out).astype(jnp.bfloat16)
    grad_down = contract_rows(back_rows, hidden)
    dhidden = jnp.dot(back_rows, down_full, preferred_element_type=jnp.float32)
    d_up = (dhidden * gated_value).astype(jnp.bfloat16)
    d_gate = (dhidden * up_value * gate_sigmoid * (1.0 + gate_value * (1.0 - gate_sigmoid))).astype(
        jnp.bfloat16
    )
    grad_gate = contract_rows(normed_two, d_gate)
    grad_up = contract_rows(normed_two, d_up)
    dnorm_two = lax.psum(
        (times_transpose(d_gate, gate_full) + times_transpose(d_up, up_full)).astype(jnp.bfloat16),
        "tensor",
    ).astype(jnp.float32)
    gain_two = jnp.sum(dnorm_two * unit_two, 0)
    dmiddle = back_rows.astype(jnp.float32) + norm_back(
        dnorm_two, norm_gains[1], unit_two, inverse_two
    )
    dmiddle_low = dmiddle.astype(jnp.bfloat16)
    grad_out = contract_rows(dmiddle_low, mixed_low)
    dmixed = jnp.dot(dmiddle_low, o_full, preferred_element_type=jnp.float32).astype(jnp.bfloat16)
    dmixed = dmixed.reshape(sequence_count, SEQUENCE_LENGTH, kv_heads, group_width, HEAD_WIDTH)
    dq_list, dk_list, dv_list = ([], [], [])
    seq_index = 0
    dquery, d_key, dvalue = attend_backward(
        query_grouped[seq_index],
        key_turned[seq_index],
        value_seqs[seq_index],
        dmixed[seq_index],
        logsum_list[seq_index],
        prefixes[seq_index],
    )
    dq_list.append(
        unrotate(dquery, cosine_values, sine_values).reshape(SEQUENCE_LENGTH, q_heads * HEAD_WIDTH)
    )
    dk_list.append(
        unrotate(d_key, cosine_values, sine_values).reshape(SEQUENCE_LENGTH, kv_heads * HEAD_WIDTH)
    )
    dv_list.append(dvalue.reshape(SEQUENCE_LENGTH, kv_heads * HEAD_WIDTH))
    dquery_low = dq_list[0].astype(jnp.bfloat16)
    dkey_low = dk_list[0].astype(jnp.bfloat16)
    dvalue_low = dv_list[0].astype(jnp.bfloat16)
    grad_q = contract_rows(first_normed_input, dquery_low)
    grad_k = contract_rows(first_normed_input, dkey_low)
    grad_v = contract_rows(first_normed_input, dvalue_low)
    dnorm_one = lax.psum(
        (
            times_transpose(dquery_low, q_full)
            + times_transpose(dkey_low, k_full)
            + times_transpose(dvalue_low, v_full)
        ).astype(jnp.bfloat16),
        "tensor",
    ).astype(jnp.float32)
    gain_one = jnp.sum(dnorm_one * unit_one, 0)
    in_grad = dmiddle + norm_back(dnorm_one, norm_gains[0], unit_one, inverse_one)
    return (
        block_out,
        in_grad,
        (
            grad_q,
            grad_k,
            grad_v,
            grad_out,
            grad_gate,
            grad_up,
            grad_down,
            jnp.stack([gain_one, gain_two]),
        ),
    )


def adam_step(weight, gradient, first_moment, second_moment, rate, decay, factor, fix_one, fix_two):
    clipped = factor * gradient
    first_new = beta_one * first_moment + (1.0 - beta_one) * clipped
    second_new = beta_two * second_moment + (1.0 - beta_two) * clipped * clipped
    update = first_new / fix_one / (jnp.sqrt(second_new / fix_two) + adam_eps) + decay * weight
    return (weight - rate * update, first_new, second_new)


def local(
    block_in,
    prefix_len,
    out_grad,
    step_count,
    q_weight,
    key_matrix,
    value_matrix,
    o_weight,
    gate_weight,
    up_weight,
    down_weight,
    norm_gains,
    query_mean_moment,
    key_mean_moment,
    value_mean_moment,
    output_mean_moment,
    gate_mean_moment,
    up_mean_moment,
    down_mean_moment,
    gains_mean_moment,
    q_second,
    key_square_moment,
    value_square_moment,
    o_second,
    gate_second,
    up_second,
    down_second,
    gains_second,
):
    q_low = q_weight.astype(jnp.bfloat16)
    key_weight_narrow = key_matrix.astype(jnp.bfloat16)
    value_weight_narrow = value_matrix.astype(jnp.bfloat16)
    o_low = o_weight.astype(jnp.bfloat16)
    gate_low = gate_weight.astype(jnp.bfloat16)
    up_low = up_weight.astype(jnp.bfloat16)
    down_low = down_weight.astype(jnp.bfloat16)
    weights = (
        lax.all_gather(q_low, "dp", axis=0, tiled=True),
        lax.all_gather(key_weight_narrow, "dp", axis=0, tiled=True),
        lax.all_gather(value_weight_narrow, "dp", axis=0, tiled=True),
        lax.all_gather(o_low, "dp", axis=0, tiled=True),
        lax.all_gather(gate_low, "dp", axis=0, tiled=True),
        lax.all_gather(up_low, "dp", axis=0, tiled=True),
        lax.all_gather(down_low, "dp", axis=0, tiled=True),
    )
    cosine_values, sine_values = rotary_tables(SEQUENCE_LENGTH, HEAD_WIDTH)
    micro_rows = SEQ_MB * SEQUENCE_LENGTH
    outputs, in_grads = ([], [])
    totals = None
    for micro_index in range(MICRO):
        input_low = block_in[micro_index * micro_rows : (micro_index + 1) * micro_rows]
        back_rows = out_grad[micro_index * micro_rows : (micro_index + 1) * micro_rows]
        prefixes = prefix_len[micro_index * SEQ_MB : (micro_index + 1) * SEQ_MB]
        block_out, in_grad, grad_list = run_micro(
            input_low, back_rows, prefixes, weights, norm_gains, cosine_values, sine_values
        )
        outputs.append(block_out)
        in_grads.append(in_grad)
        grad_list = tuple(grad_list)
        totals = (
            grad_list
            if totals is None
            else tuple((earlier + later for earlier, later in zip(totals, grad_list)))
        )
    grad_q, grad_k, grad_v, grad_out, grad_gate, grad_up, grad_down, grad_gains = totals
    reduced = (
        lax.psum_scatter(grad_q, "dp", scatter_dimension=0, tiled=True),
        lax.psum_scatter(grad_k, "dp", scatter_dimension=0, tiled=True),
        lax.psum_scatter(grad_v, "dp", scatter_dimension=0, tiled=True),
        lax.psum_scatter(grad_out, "dp", scatter_dimension=0, tiled=True),
        lax.psum_scatter(grad_gate, "dp", scatter_dimension=0, tiled=True),
        lax.psum_scatter(grad_up, "dp", scatter_dimension=0, tiled=True),
        lax.psum_scatter(grad_down, "dp", scatter_dimension=0, tiled=True),
        lax.psum_scatter(grad_gains, "dp", scatter_dimension=1, tiled=True),
    )
    squares = sum((jnp.sum(jnp.square(grad_share)) for grad_share in reduced[:7])) + 0.5 * jnp.sum(
        jnp.square(reduced[7])
    )
    total_square = lax.psum(squares, ("dp", "tensor"))
    grad_norm = jnp.sqrt(total_square)
    factor = jnp.minimum(1.0, clip_limit / grad_norm)
    step_float = step_count[0].astype(jnp.float32)
    fix_one = 1.0 - jnp.power(beta_one, step_float)
    fix_two = 1.0 - jnp.power(beta_two, step_float)
    gain_width = norm_gains.shape[1] // lax.axis_size("dp")
    old_gains = lax.dynamic_slice_in_dim(
        norm_gains, lax.axis_index("dp") * gain_width, gain_width, 1
    )
    masters = (
        q_weight,
        key_matrix,
        value_matrix,
        o_weight,
        gate_weight,
        up_weight,
        down_weight,
        old_gains,
    )
    firsts = (
        query_mean_moment,
        key_mean_moment,
        value_mean_moment,
        output_mean_moment,
        gate_mean_moment,
        up_mean_moment,
        down_mean_moment,
        gains_mean_moment,
    )
    seconds = (
        q_second,
        key_square_moment,
        value_square_moment,
        o_second,
        gate_second,
        up_second,
        down_second,
        gains_second,
    )
    rate_list = matrix_rates + (gain_rate,)
    decay_list = (decay_rate,) * 7 + (0.0,)
    new_weights, new_firsts, new_seconds = ([], [], [])
    for weight, gradient, first_moment, second_moment, rate, decay in zip(
        masters, reduced, firsts, seconds, rate_list, decay_list
    ):
        weight_new, first_new, second_new = adam_step(
            weight, gradient, first_moment, second_moment, rate, decay, factor, fix_one, fix_two
        )
        new_weights.append(weight_new)
        new_firsts.append(first_new)
        new_seconds.append(second_new)
    return (
        jnp.concatenate(outputs, 0),
        jnp.concatenate(in_grads, 0),
        grad_norm.reshape(1),
        new_weights[0],
        new_weights[1],
        new_weights[2],
        new_weights[3],
        new_weights[4],
        new_weights[5],
        new_weights[6],
        new_weights[7],
        new_firsts[0],
        new_firsts[1],
        new_firsts[2],
        new_firsts[3],
        new_firsts[4],
        new_firsts[5],
        new_firsts[6],
        new_firsts[7],
        new_seconds[0],
        new_seconds[1],
        new_seconds[2],
        new_seconds[3],
        new_seconds[4],
        new_seconds[5],
        new_seconds[6],
        new_seconds[7],
    )


def solution(mesh):
    return jax.shard_map(
        local,
        mesh=mesh,
        in_specs=(
            P("dp", None),
            P("dp"),
            P("dp", None),
            P(),
            P("dp", "tensor"),
            P("dp", "tensor"),
            P("dp", "tensor"),
            P("dp", "tensor"),
            P("dp", "tensor"),
            P("dp", "tensor"),
            P("dp", "tensor"),
            P(),
            P("dp", "tensor"),
            P("dp", "tensor"),
            P("dp", "tensor"),
            P("dp", "tensor"),
            P("dp", "tensor"),
            P("dp", "tensor"),
            P("dp", "tensor"),
            P(None, "dp"),
            P("dp", "tensor"),
            P("dp", "tensor"),
            P("dp", "tensor"),
            P("dp", "tensor"),
            P("dp", "tensor"),
            P("dp", "tensor"),
            P("dp", "tensor"),
            P(None, "dp"),
        ),
        out_specs=(
            P("dp", None),
            P("dp", None),
            P(),
            P("dp", "tensor"),
            P("dp", "tensor"),
            P("dp", "tensor"),
            P("dp", "tensor"),
            P("dp", "tensor"),
            P("dp", "tensor"),
            P("dp", "tensor"),
            P(None, "dp"),
            P("dp", "tensor"),
            P("dp", "tensor"),
            P("dp", "tensor"),
            P("dp", "tensor"),
            P("dp", "tensor"),
            P("dp", "tensor"),
            P("dp", "tensor"),
            P(None, "dp"),
            P("dp", "tensor"),
            P("dp", "tensor"),
            P("dp", "tensor"),
            P("dp", "tensor"),
            P("dp", "tensor"),
            P("dp", "tensor"),
            P("dp", "tensor"),
            P(None, "dp"),
        ),
        check_vma=False,
    )
```

profile of v0, /device:TPU:0, one launch (start us, length us, event | category | flops | bytes accessed | tf_op | source)
XLA Modules:
  0.0 2582.4 jit_solution(10935778273474949260)
XLA Ops:
  20.4 49.9 %all-gather.10.cloned.1.call-done = bf16[1536,384]{1,0:T(8,128)(2,1)} async-done(((bf16[96,384]{1,0:T(8,128)(2,1)}), bf16[1536,384]{1,0:T(8,128)(2,1)}) %all-gather.10.cloned.1.call-update) | async-done | bytes 1179664 | tf_op jit(solution)/shard_map/all_gather | solution.py:341
  78.0 50.7 %all-gather.12.cloned.1.call-done = bf16[1536,384]{1,0:T(8,128)(2,1)} async-done(((bf16[96,384]{1,0:T(8,128)(2,1)}), bf16[1536,384]{1,0:T(8,128)(2,1)}) %all-gather.12.cloned.1.call-update) | async-done | bytes 1179664 | tf_op jit(solution)/shard_map/all_gather | solution.py:342
  137.8 55.5 %all-gather.8.cloned.1.call-done = bf16[1536,768]{1,0:T(8,128)(2,1)} async-done(((bf16[96,768]{1,0:T(8,128)(2,1)}), bf16[1536,768]{1,0:T(8,128)(2,1)}) %all-gather.8.cloned.1.call-update) | async-done | bytes 2359312 | tf_op jit(solution)/shard_map/all_gather | solution.py:340
  211.3 32.9 %while.54 = (s32[]{:T(128)}, bf16[2,512,4,2,96]{1,4,3,2,0:T(8,128)(2,1)}, f32[2,4,2,512]{3,2,1,0:T(2,128)}, s32[2]{0:T(128)S(1)}, s32[]{:T(128)}, /*index=5*/bf1...) while((s32[]{:T(128)}, ...), condition=%wide.region_4.5_spmd, body=%wide.region_1.4_spmd.sunk | while | flops 1661990400 | bytes 59645140 | solution.py:145
  246.1 35.6 %while.55 = (s32[]{:T(128)}, bf16[2,512,4,2,96]{1,4,3,2,0:T(8,128)(2,1)}, f32[2,4,2,512]{3,2,1,0:T(2,128)S(1)}, s32[2]{0:T(128)S(1)}, s32[]{:T(128)}, /*index=5*...) while((s32[]{:T(128)}, ...), condition=%wide.region_12.13_spmd, body=%wide.region_9.12_spmd.sunk | while | flops 1661990400 | bytes 72227096 | solution.py:145
  301.8 27.3 %all-reduce.11.cloned.1.call-done = (bf16[1024,1536]{1,0:T(8,128)(2,1)}, bf16[1024,1536]{1,0:T(8,128)(2,1)}) async-done(((bf16[1024,1536]{1,0:T(8,128)(2,1)}, bf16[1024,1536]{1,0:T(8,128)(2,1)}), (bf16[1024,1536]{1,0:T(8,128)(2,1)}, bf16[1024,1536]{1,0:T(8,128)(2,1)})) %all-reduce.11.cloned.1.call-update) | async-done | bytes 6291472 | tf_op jit(solution)/shard_map/psum | solution.py:210
  340.9 87.1 %all-gather.16.cloned.1.call-done = bf16[1536,2048]{1,0:T(8,128)(2,1)} async-done(((bf16[96,2048]{1,0:T(8,128)(2,1)}), bf16[1536,2048]{1,0:T(8,128)(2,1)}) %all-gather.16.cloned.1.call-update) | async-done | bytes 6291472 | tf_op jit(solution)/shard_map/all_gather | solution.py:344
  428.0 11.7 fusion.172
  439.7 84.5 %all-gather.18.cloned.1.call-done = bf16[1536,2048]{1,0:T(8,128)(2,1)} async-done(((bf16[96,2048]{1,0:T(8,128)(2,1)}), bf16[1536,2048]{1,0:T(8,128)(2,1)}) %all-gather.18.cloned.1.call-update) | async-done | bytes 6291472 | tf_op jit(solution)/shard_map/all_gather | solution.py:345
  524.3 11.9 fusion.173
  554.1 66.3 %all-gather.20.cloned.1.call-done = bf16[1536,2048]{1,0:T(8,128)(2,1)} async-done(((bf16[96,2048]{1,0:T(8,128)(2,1)}), bf16[1536,2048]{1,0:T(8,128)(2,1)}) %all-gather.20.cloned.1.call-update) | async-done | bytes 6291472 | tf_op jit(solution)/shard_map/all_gather | solution.py:346
  620.4 19.4 multiply_convert_fusion.2
  639.8 11.9 fusion.176
  651.7 16.8 multiply_convert_fusion
  668.5 10.7 fusion.179
  679.1 11.4 add_convert_fusion.3
  698.8 11.6 convolution_convert_fusion.1
  710.4 10.4 convolution_convert_fusion
  754.2 171.2 %while.57 = (s32[]{:T(128)}, f32[1024,4,96]{0,2,1:T(8,128)}, f32[1024,4,96]{0,2,1:T(8,128)}, f32[2,512,4,2,96]{1,0,4,3,2:T(2,128)}, s32[2]{0:T(128)S(1)}, /*inde...) while((s32[]{:T(128)}, f32[1024,4,96]{0,2,1:T(8,128)}, ...), condition=%wide.region_27.28_spmd.clone, body=%wide.region_25.27_spmd.clone.sunk | while | flops 4067685888 | bytes 192764240 | solution.py:168
  766.3 13.0 fusion.310
  779.3 11.3 fusion.311
  795.6 28.8 %dynamic_update_slice.37 = f32[2,512,4,2,96]{1,0,4,3,2:T(2,128)} dynamic-update-slice(f32[2,512,4,2,96]{1,0,4,3,2:T(2,128)} %get-tuple-element.880, f32[1,512,4,2,96]{1,0,4,3,2:T(1,128)S(1)} %copy.122, s32[]{:T(128)} %get-tuple-element.877, s32[]{:T(128)} %constant.89.clone.1..sunk.3, s32[]{:T(128)} %constant.89.clone.1..sunk.3, s32[]{:T(128)} %constant.89.clone.1..sunk.3, s32[]{:T(128)} %constant.89.clone.1..sunk.3) | dynamic-update-slice | bytes 3145732 | tf_op jit(solution)/shard_map/while/body/jit(dynamic_update_index_in_dim)/dynamic_update_slice | solution.py:145
  851.5 13.0 fusion.310
  864.5 11.3 fusion.311
  880.8 28.8 %dynamic_update_slice.37 = f32[2,512,4,2,96]{1,0,4,3,2:T(2,128)} dynamic-update-slice(f32[2,512,4,2,96]{1,0,4,3,2:T(2,128)} %get-tuple-element.880, f32[1,512,4,2,96]{1,0,4,3,2:T(1,128)S(1)} %copy.122, s32[]{:T(128)} %get-tuple-element.877, s32[]{:T(128)} %constant.89.clone.1..sunk.3, s32[]{:T(128)} %constant.89.clone.1..sunk.3, s32[]{:T(128)} %constant.89.clone.1..sunk.3, s32[]{:T(128)} %constant.89.clone.1..sunk.3) | dynamic-update-slice | bytes 3145732 | tf_op jit(solution)/shard_map/while/body/jit(dynamic_update_index_in_dim)/dynamic_update_slice | solution.py:145
  935.6 172.8 %while.56 = (s32[]{:T(128)}, f32[1024,4,96]{0,2,1:T(8,128)}, f32[1024,4,96]{0,2,1:T(8,128)}, f32[2,512,4,2,96]{1,0,4,3,2:T(2,128)}, s32[2]{0:T(128)S(1)}, /*inde...) while((s32[]{:T(128)}, f32[1024,4,96]{0,2,1:T(8,128)}, ...), condition=%wide.region_20.21_spmd.clone, body=%wide.region_18.20_spmd.clone.sunk | while | flops 4067685888 | bytes 192764240 | solution.py:168
  948.1 12.9 fusion.298
  961.0 11.3 fusion.299
  977.4 28.8 %dynamic_update_slice.36 = f32[2,512,4,2,96]{1,0,4,3,2:T(2,128)} dynamic-update-slice(f32[2,512,4,2,96]{1,0,4,3,2:T(2,128)} %get-tuple-element.835, f32[1,512,4,2,96]{1,0,4,3,2:T(1,128)S(1)} %copy.121, s32[]{:T(128)} %get-tuple-element.832, s32[]{:T(128)} %constant.89.clone.1..sunk.2, s32[]{:T(128)} %constant.89.clone.1..sunk.2, s32[]{:T(128)} %constant.89.clone.1..sunk.2, s32[]{:T(128)} %constant.89.clone.1..sunk.2) | dynamic-update-slice | bytes 3145732 | tf_op jit(solution)/shard_map/while/body/jit(dynamic_update_index_in_dim)/dynamic_update_slice | solution.py:145
  1034.0 12.9 fusion.298
  1047.0 11.3 fusion.299
  1063.3 28.8 %dynamic_update_slice.36 = f32[2,512,4,2,96]{1,0,4,3,2:T(2,128)} dynamic-update-slice(f32[2,512,4,2,96]{1,0,4,3,2:T(2,128)} %get-tuple-element.835, f32[1,512,4,2,96]{1,0,4,3,2:T(1,128)S(1)} %copy.121, s32[]{:T(128)} %get-tuple-element.832, s32[]{:T(128)} %constant.89.clone.1..sunk.2, s32[]{:T(128)} %constant.89.clone.1..sunk.2, s32[]{:T(128)} %constant.89.clone.1..sunk.2, s32[]{:T(128)} %constant.89.clone.1..sunk.2) | dynamic-update-slice | bytes 3145732 | tf_op jit(solution)/shard_map/while/body/jit(dynamic_update_index_in_dim)/dynamic_update_slice | solution.py:145
  1207.0 11.4 fusion.182
  1226.9 13.7 convolution_add_fusion.1
  1240.9 9.9 fusion.183
  1260.7 9.9 fusion.113
  1270.6 12.2 add_bitcast_fusion
  1283.7 57.5 %reduce-scatter.15.cloned.1.call-done = f32[96,384]{1,0:T(8,128)} async-done(((f32[1536,384]{1,0:T(8,128)}), f32[96,384]{1,0:T(8,128)}) %reduce-scatter.15.cloned.1.call-update) | async-done | bytes 147472 | tf_op jit(solution)/shard_map/reduce_scatter | solution.py:371
  1342.7 131.6 %reduce-scatter.13.cloned.1.call-done = f32[96,384]{1,0:T(8,128)} async-done(((f32[1536,384]{1,0:T(8,128)}), f32[96,384]{1,0:T(8,128)}) %reduce-scatter.13.cloned.1.call-update) | async-done | bytes 147472 | tf_op jit(solution)/shard_map/reduce_scatter | solution.py:370
  1475.9 140.2 %reduce-scatter.11.cloned.1.call-done = f32[96,768]{1,0:T(8,128)} async-done(((f32[1536,768]{1,0:T(8,128)}), f32[96,768]{1,0:T(8,128)}) %reduce-scatter.11.cloned.1.call-update) | async-done | bytes 294928 | tf_op jit(solution)/shard_map/reduce_scatter | solution.py:369
  1619.7 138.8 %reduce-scatter.17.cloned.1.call-done = f32[96,768]{1,0:T(8,128)} async-done(((f32[1536,768]{1,0:T(8,128)}), f32[96,768]{1,0:T(8,128)}) %reduce-scatter.17.cloned.1.call-update) | async-done | bytes 294928 | tf_op jit(solution)/shard_map/reduce_scatter | solution.py:372
  1760.8 20.1 fusion.86
  1781.0 10.9 pad_maximum_fusion
  1791.8 93.0 %reduce-scatter.25.cloned.1.call-done = f32[96,2]{1,0:T(8,128)} async-done(((f32[1536,2]{1,0:T(8,128)}), f32[96,2]{1,0:T(8,128)}) %reduce-scatter.25.cloned.1.call-update) | async-done | bytes 784
  1886.9 206.5 %reduce-scatter.19.cloned.1.call-done = f32[96,2048]{1,0:T(8,128)} async-done(((f32[1536,2048]{1,0:T(8,128)}), f32[96,2048]{1,0:T(8,128)}) %reduce-scatter.19.cloned.1.call-update) | async-done | bytes 786448 | tf_op jit(solution)/shard_map/reduce_scatter | solution.py:373
  2096.0 207.5 %reduce-scatter.21.cloned.1.call-done = f32[96,2048]{1,0:T(8,128)} async-done(((f32[1536,2048]{1,0:T(8,128)}), f32[96,2048]{1,0:T(8,128)}) %reduce-scatter.21.cloned.1.call-update) | async-done | bytes 786448 | tf_op jit(solution)/shard_map/reduce_scatter | solution.py:374
  2306.1 206.5 %reduce-scatter.23.cloned.1.call-done = f32[96,2048]{1,0:T(8,128)} async-done(((f32[1536,2048]{1,0:T(8,128)}), f32[96,2048]{1,0:T(8,128)}) %reduce-scatter.23.cloned.1.call-update) | async-done | bytes 786448 | tf_op jit(solution)/shard_map/reduce_scatter | solution.py:375
  2520.2 40.4 %psum.71 = f32[]{:T(128)} all-reduce(f32[]{:T(128)S(6)} %add.445), channel_id=1, replica_groups=mesh['dp'=16,'tensor'=2] {'dp','tensor'}, use_global_device_ids=true, to_apply=%region_50.51 | all-reduce | flops 1 | bytes 8 | tf_op jit(solution)/shard_map/psum | solution.py:381
  (501 shorter events, 492.0 us)
Async XLA Ops:
  7.2 63.1 %all-gather.10.cloned.1.call-start = ((), (), s32[]{:S(2)}) async-start(), calls=%async_computation.9 | async-start | bytes 1253376 | tf_op jit(solution)/shard_map/all_gather | solution.py:341
  8.8 119.9 %all-gather.12.cloned.1.call-start = ((), (), s32[]{:S(2)}) async-start(), calls=%async_computation.10 | async-start | bytes 1253376 | tf_op jit(solution)/shard_map/all_gather | solution.py:342
  10.5 182.8 %all-gather.8.cloned.1.call-start = ((), (), s32[]{:S(2)}) async-start(), calls=%async_computation.8 | async-start | bytes 2506752 | tf_op jit(solution)/shard_map/all_gather | solution.py:340
  12.2 275.2 %all-gather.14.cloned.1.call-start = ((), (), s32[]{:S(2)}) async-start(), calls=%async_computation.11 | async-start | bytes 2506752 | tf_op jit(solution)/shard_map/all_gather | solution.py:343
  13.9 315.2 %all-reduce.11.cloned.1.call-start = ((), (), s32[]{:S(2)}) async-start(), calls=%async_computation.25 | async-start | bytes 12582912 | tf_op jit(solution)/shard_map/psum | solution.py:210
  15.4 183.9 %copy-start.88 = (f32[1536]{0:T(1024)}, f32[1536]{0:T(1024)S(1)}, u32[]{:S(2)}) copy-start(f32[1536]{0:T(1024)S(1)} %get-tuple-element.330) | copy-start | bytes 18436
  20.3 173.0 %copy-start.96 = (f32[1024]{0:T(1024)}, f32[1024]{0:T(1024)S(1)}, u32[]{:S(2)}) copy-start(f32[1024]{0:T(1024)S(1)} %get-tuple-element.494) | copy-start | bytes 12292
  20.3 179.1 %copy-start.94 = (f32[1024]{0:T(1024)}, f32[1024]{0:T(1024)S(1)}, u32[]{:S(2)}) copy-start(f32[1024]{0:T(1024)S(1)} %get-tuple-element.493) | copy-start | bytes 12292
  20.3 54.1 %slice-start = ((s8[6291456]{0:T(1024)(128)(4,1)}), s8[2097152]{0:T(1024)(128)(4,1)S(1)}, s32[]{:S(2)}) async-start(s8[6291456]{0:T(1024)(128)(4,1)} %bitcast.382), calls=%async_computation.26 | async-start | bytes 4194304
  20.4 55.8 %copy-start.32 = (f32[1024,96]{0,1:T(8,128)}, f32[1024,96]{0,1:T(8,128)S(1)}, u32[]{:S(2)}) copy-start(f32[1024,96]{0,1:T(8,128)S(1)} %get-tuple-element.495) | copy-start | bytes 1179652
  20.4 185.7 %copy-start.30 = (f32[1024,96]{0,1:T(8,128)}, f32[1024,96]{0,1:T(8,128)S(1)}, u32[]{:S(2)}) copy-start(f32[1024,96]{0,1:T(8,128)S(1)} %get-tuple-element.496) | copy-start | bytes 1179652
  211.3 34.3 %copy-start.4 = (bf16[1024,4,96]{0,2,1:T(8,128)(2,1)S(1)}, bf16[1024,4,96]{0,2,1:T(8,128)(2,1)}, u32[]{:S(2)}) copy-start(bf16[1024,4,96]{0,2,1:T(8,128)(2,1)} %get-tuple-element.869) | copy-start | bytes 2359300
  298.0 130.0 %all-gather.16.cloned.1.call-start = ((), (), s32[]{:S(2)}) async-start(), calls=%async_computation.12 | async-start | bytes 6684672 | tf_op jit(solution)/shard_map/all_gather | solution.py:344
  300.0 224.3 %all-gather.18.cloned.1.call-start = ((), (), s32[]{:S(2)}) async-start(), calls=%async_computation.13 | async-start | bytes 6684672 | tf_op jit(solution)/shard_map/all_gather | solution.py:345
  300.8 319.6 %all-gather.20.cloned.1.call-start = ((), (), s32[]{:S(2)}) async-start(), calls=%async_computation.14 | async-start | bytes 6684672 | tf_op jit(solution)/shard_map/all_gather | solution.py:346
  301.7 427.5 %all-reduce.9.cloned.1.call-start = ((), (), s32[]{:S(2)}) async-start(), calls=%async_computation.24 | async-start | bytes 12582912 | tf_op jit(solution)/shard_map/psum | solution.py:233
  340.9 204.2 %copy-start.49 = (bf16[1024,1536]{1,0:T(8,128)(2,1)}, bf16[1024,1536]{1,0:T(8,128)(2,1)S(1)}, u32[]{:S(2)}) copy-start(bf16[1024,1536]{1,0:T(8,128)(2,1)S(1)} %get-tuple-element.458) | copy-start | bytes 9437188
  524.3 11.9 copy-start.104
  524.3 20.8 slice-start.6
  639.8 11.9 copy-start.103
  668.5 22.1 slice-start.8
  679.1 11.4 slice-start.9
  679.1 11.4 copy-start.109
  698.7 519.8 %all-reduce.7.cloned.1.call-start = ((), (), s32[]{:S(2)}) async-start(), calls=%async_computation.23 | async-start | bytes 25165824 | tf_op jit(solution)/shard_map/psum | solution.py:221
  698.8 11.6 copy-start.112
  710.4 18.8 copy-start.7
  710.4 18.8 copy-start.87
  710.4 18.8 copy-start.91
  710.4 18.8 copy-start.93
  935.6 172.8 %copy-start.31 = (f32[1024,96]{0,1:T(8,128)S(1)}, f32[1024,96]{0,1:T(8,128)}, u32[]{:S(2)}) copy-start(f32[1024,96]{0,1:T(8,128)} %copy-done.30) | copy-start | bytes 1179652
  1155.5 185.7 %reduce-scatter.15.cloned.1.call-start = ((), (), s32[]{:S(2)}) async-start(), calls=%async_computation.17 | async-start | bytes 2506752 | tf_op jit(solution)/shard_map/reduce_scatter | solution.py:371
  1165.7 308.7 %reduce-scatter.13.cloned.1.call-start = ((), (), s32[]{:S(2)}) async-start(), calls=%async_computation.16 | async-start | bytes 2506752 | tf_op jit(solution)/shard_map/reduce_scatter | solution.py:370
  1177.2 438.9 %reduce-scatter.11.cloned.1.call-start = ((), (), s32[]{:S(2)}) async-start(), calls=%async_computation.15 | async-start | bytes 5013504 | tf_op jit(solution)/shard_map/reduce_scatter | solution.py:369
  1189.6 568.9 %reduce-scatter.17.cloned.1.call-start = ((), (), s32[]{:S(2)}) async-start(), calls=%async_computation.18 | async-start | bytes 5013504 | tf_op jit(solution)/shard_map/reduce_scatter | solution.py:372
  1205.2 13.2 copy-start.99
  1205.2 13.2 copy-start.98
  1205.2 679.6 %reduce-scatter.25.cloned.1.call-start = ((), (), s32[]{:S(2)}) async-start(), calls=%async_computation.22 | async-start | bytes 835584
  1226.9 866.6 %reduce-scatter.19.cloned.1.call-start = ((), (), s32[]{:S(2)}) async-start(), calls=%async_computation.19 | async-start | bytes 13369344 | tf_op jit(solution)/shard_map/reduce_scatter | solution.py:373
  1240.7 1062.8 %reduce-scatter.21.cloned.1.call-start = ((), (), s32[]{:S(2)}) async-start(), calls=%async_computation.20 | async-start | bytes 13369344 | tf_op jit(solution)/shard_map/reduce_scatter | solution.py:374
  1260.6 1251.9 %reduce-scatter.23.cloned.1.call-start = ((), (), s32[]{:S(2)}) async-start(), calls=%async_computation.21 | async-start | bytes 13369344 | tf_op jit(solution)/shard_map/reduce_scatter | solution.py:375
  1282.8 478.0 %copy-start.8 = (bf16[1024,1536]{1,0:T(8,128)(2,1)S(1)}, bf16[1024,1536]{1,0:T(8,128)(2,1)}, u32[]{:S(2)}) copy-start(bf16[1024,1536]{1,0:T(8,128)(2,1)} %get-tuple-element.413) | copy-start | bytes 9437188
  1780.9 734.2 %copy-start.27 = (bf16[1024,1536]{1,0:T(8,128)(2,1)S(1)}, bf16[1024,1536]{1,0:T(8,128)(2,1)}, u32[]{:S(2)}) copy-start(bf16[1024,1536]{1,0:T(8,128)(2,1)} %get-tuple-element.459) | copy-start | bytes 9437188
  2515.2 46.2 %copy-start.101 = (f32[2,96]{1,0:T(2,128)S(1)}, f32[2,96]{1,0:T(2,128)}, u32[]{:S(2)}) copy-start(f32[2,96]{1,0:T(2,128)} %param.63) | copy-start | bytes 2308
  2515.2 46.2 %copy-start.102 = (f32[2,96]{1,0:T(2,128)S(1)}, f32[2,96]{1,0:T(2,128)}, u32[]{:S(2)}) copy-start(f32[2,96]{1,0:T(2,128)} %param.55) | copy-start | bytes 2308
  2520.2 46.3 %copy-start.44 = (f32[96,2048]{1,0:T(8,128)S(1)}, f32[96,2048]{1,0:T(8,128)}, u32[]{:S(2)}) copy-start(f32[96,2048]{1,0:T(8,128)} %param.45) | copy-start | bytes 2359300
  2520.2 46.3 %copy-start.48 = (f32[96,2048]{1,0:T(8,128)S(1)}, f32[96,2048]{1,0:T(8,128)}, u32[]{:S(2)}) copy-start(f32[96,2048]{1,0:T(8,128)} %reduce-scatter.21.cloned.1.call-done) | copy-start | bytes 2359300
  2520.2 46.3 %copy-start.68 = (f32[96,2048]{1,0:T(8,128)S(1)}, f32[96,2048]{1,0:T(8,128)}, u32[]{:S(2)}) copy-start(f32[96,2048]{1,0:T(8,128)} %param.61) | copy-start | bytes 2359300
  2520.2 46.3 %copy-start.69 = (f32[96,2048]{1,0:T(8,128)S(1)}, f32[96,2048]{1,0:T(8,128)}, u32[]{:S(2)}) copy-start(f32[96,2048]{1,0:T(8,128)} %param.53) | copy-start | bytes 2359300
  (104 other events, 478.6 us)
Sparse Core Ops, SparseCore 0:
  11.4 58.8 all-gather.9
  73.7 54.9 all-gather.11
  132.1 61.1 all-gather.7
  196.5 61.1 all-gather.13
  298.2 30.8 all-reduce.10
  332.7 95.2 all-gather.15
  431.8 92.4 all-gather.17
  528.0 92.4 all-gather.19
  698.8 30.3 all-reduce.8
  1155.6 50.9 all-reduce.6
  1211.5 129.6 reduce-scatter.14
  1346.7 127.5 reduce-scatter.12
  1479.5 136.5 reduce-scatter.10
  1622.0 136.4 reduce-scatter.16
  1763.6 121.1 reduce-scatter.24
  1890.3 203.0 reduce-scatter.18
  2099.9 203.5 reduce-scatter.20
  2309.0 203.4 reduce-scatter.22
where the time goes:
time: 2600 us; the launch traced here: 2580 us
  waiting for transfers between devices  1610 us (62%)
  matrix products  514 us (20%)
  other arithmetic  201 us (8%)
  local copies, waits for them, and re-layouts  182 us (7%)
  blocking collectives  40.4 us (2%)
    reduce_scatter x1, waiting for transfers between devices, local(): lax.psum_scatter(grad_up, 'dp', scatter_dimension=0, tiled=True)  207 us
    reduce_scatter x1, waiting for transfers between devices, local(): lax.psum_scatter(grad_gate, 'dp', scatter_dimension=0, tiled=True)  206 us
    reduce_scatter x1, waiting for transfers between devices, local(): lax.psum_scatter(grad_down, 'dp', scatter_dimension=0, tiled=True)  206 us
    reduce_scatter x1, waiting for transfers between devices, local(): lax.psum_scatter(grad_q, 'dp', scatter_dimension=0, tiled=True)  140 us
    reduce_scatter x1, waiting for transfers between devices, local(): lax.psum_scatter(grad_out, 'dp', scatter_dimension=0, tiled=True)  139 us
    reduce_scatter x1, waiting for transfers between devices, local(): lax.psum_scatter(grad_k, 'dp', scatter_dimension=0, tiled=True)  132 us
    dynamic_update_slice x8, local copies, waits for them, and re-layouts, attend_forward(): return lax.map(one_block, jnp.arange(block_list, dtype=jnp.int32))  122 us
    dot_general x14, matrix products, contract_rows(): lax.dot_general(left_side, right_side, (((0,), (0,)), ((), ())), preferre...  114 us
  transfers between devices with their start and end apart: 18, of which 16 were waited for; matrix products, arithmetic and copies ran while one was open for 14% of the time, Pallas kernels for 0%

commit v1 on v0

v1 whole, which is shorter than its diff:
```python
import functools
import math

import jax
import jax.numpy as jnp
from jax import lax
from jax.experimental import pallas as pl
from jax.experimental.pallas import tpu as pltpu
from jax.sharding import PartitionSpec as P

HEAD_WIDTH = 96
GROUP_WIDTH = 2
SEQUENCE_LENGTH = 1024
QUERY_CHUNK = 512
VMEM_BYTES = 58 * 2**20
LOG2_E = 1.4426950408889634
SCORE_SCALE = 1.0 / math.sqrt(HEAD_WIDTH)

theta_base = 100000.0
norm_eps = 1e-05
beta_one = 0.9
beta_two = 0.95
adam_eps = 1e-08
decay_rate = 0.1
clip_limit = 1.0
neg_fill = -1e30
matrix_rates = (0.08, 0.08, 0.08, 1.0, 0.08, 0.08, 0.1)
gain_rate = 1.0

BF16 = jnp.bfloat16
F32 = jnp.float32
ANYWHERE = pl.BlockSpec(memory_space=pl.ANY)
MESH_ID = pl.DeviceIdType.MESH
GATHER_ORDERS = ((0, 1, 2), (2, 0, 1))
SCATTER_ORDERS = ((2, 1, 0), (1, 0, 2))
CHUNK = 256


def factor(count):
    return {16: (4, 2, 2), 64: (4, 4, 4)}.get(count, (count, 1, 1))


class Place:
    def __init__(self, dims):
        self.dims = dims
        mine = lax.axis_index("dp")
        n0, n1, n2 = dims
        self.at = (lax.rem(mine // (n1 * n2), n0), lax.rem(mine // n2, n1), lax.rem(mine, n2))

    def peer(self, dim, step):
        return lax.rem(self.at[dim] + step, self.dims[dim])

    def device(self, dim, coord):
        digits = list(self.at)
        digits[dim] = coord
        return {"dp": (digits[0] * self.dims[1] + digits[1]) * self.dims[2] + digits[2]}


def view(ref, fixed, columns):
    picks = tuple(fixed.get(d, slice(None)) for d in range(3))
    return ref.at[picks + (slice(None), pl.ds(columns[0], columns[1]))]


def entry_barrier(place):
    barrier = pltpu.get_barrier_semaphore()
    total = 0
    for dim in range(3):
        for step in range(1, place.dims[dim]):
            pl.semaphore_signal(
                barrier,
                inc=1,
                device_id=place.device(dim, place.peer(dim, step)),
                device_id_type=MESH_ID,
            )
            total += 1
    pl.semaphore_wait(barrier, total)


class GatherChunk:
    def __init__(self, place, shard, full, columns, order, send, recv, local):
        self.place, self.shard, self.full, self.columns = place, shard, full, columns
        self.order, self.send, self.recv, self.local = order, send, recv, local

    def copies(self, stage, arriving):
        place, dim, made = self.place, self.order[stage], []
        for step in range(1, place.dims[dim]):
            fixed = {d: place.at[d] for d in self.order[stage:]}
            if arriving:
                fixed[dim] = place.peer(dim, place.dims[dim] - step)
            target = view(self.full, fixed, self.columns)
            source = target
            if stage == 0 and not arriving:
                source = self.shard.at[:, pl.ds(*self.columns)]
            made.append(
                pltpu.make_async_remote_copy(
                    src_ref=source,
                    dst_ref=target,
                    send_sem=self.send.at[stage, step - 1],
                    recv_sem=self.recv.at[stage, step - 1],
                    device_id=place.device(dim, place.peer(dim, step)),
                    device_id_type=MESH_ID,
                )
            )
        return made

    def own(self):
        fixed = {d: self.place.at[d] for d in range(3)}
        return pltpu.make_async_copy(
            self.shard.at[:, pl.ds(*self.columns)],
            view(self.full, fixed, self.columns),
            self.local,
        )

    def act(self, phase):
        if phase == 0:
            self.own().start()
        else:
            if phase == 1:
                self.own().wait()
            for copy in self.copies(phase - 1, True):
                copy.wait_recv()
        if phase < 3:
            for copy in self.copies(phase, False):
                copy.start()
        else:
            for stage in range(3):
                for copy in self.copies(stage, False):
                    copy.wait_send()


class ScatterChunk:
    def __init__(self, place, grad, out, columns, order, buffers, send, recv, local):
        self.place, self.grad, self.out, self.columns = place, grad, out, columns
        self.order, self.send, self.recv, self.local = order, send, recv, local
        self.total, self.landings = buffers[0], buffers[1:]
        self.rest = [d for d in range(3) if d != order[0]]

    def pick(self, second, third):
        return tuple(second if d == self.order[1] else third for d in self.rest)

    def copies(self, stage, arriving):
        place, dim, made = self.place, self.order[stage], []
        for step in range(1, place.dims[dim]):
            to = place.peer(dim, step)
            land = self.landings[stage].at[step - 1]
            if arriving:
                source = land
            elif stage == 0:
                source = view(self.grad, {dim: to}, self.columns)
            elif stage == 1:
                source = self.total.at[self.pick(to, slice(None))]
            else:
                source = self.total.at[self.pick(place.at[self.order[1]], to)]
            made.append(
                pltpu.make_async_remote_copy(
                    src_ref=source,
                    dst_ref=land,
                    send_sem=self.send.at[stage, step - 1],
                    recv_sem=self.recv.at[stage, step - 1],
                    device_id=place.device(dim, to),
                    device_id_type=MESH_ID,
                )
            )
        return made

    def own(self):
        first = self.order[0]
        return pltpu.make_async_copy(
            view(self.grad, {first: self.place.at[first]}, self.columns), self.total, self.local
        )

    def act(self, phase):
        place, order = self.place, self.order
        if phase == 0:
            self.own().start()
        else:
            for copy in self.copies(phase - 1, True):
                copy.wait_recv()
        if phase == 1:
            self.own().wait()
            outer, inner = (place.dims[d] for d in self.rest)

            def add_first(item, carry):
                i, j = item // inner, lax.rem(item, inner)
                value = self.total[i, j].astype(F32)
                for slot in range(place.dims[order[0]] - 1):
                    value = value + self.landings[0][slot, i, j].astype(F32)
                self.total[i, j] = value.astype(BF16)
                return carry

            lax.fori_loop(0, outer * inner, add_first, 0)
        if phase == 2:

            def add_second(item, carry):
                spot = self.pick(place.at[order[1]], item)
                value = self.total[spot].astype(F32)
                for slot in range(place.dims[order[1]] - 1):
                    value = value + self.landings[1][slot, item].astype(F32)
                self.total[spot] = value.astype(BF16)
                return carry

            lax.fori_loop(0, place.dims[order[2]], add_second, 0)
        if phase < 3:
            for copy in self.copies(phase, False):
                copy.start()
        else:
            value = self.total[self.pick(place.at[order[1]], place.at[order[2]])].astype(F32)
            for slot in range(place.dims[order[2]] - 1):
                value = value + self.landings[2][slot].astype(F32)
            self.out[:, self.columns[0] : self.columns[0] + self.columns[1]] = value
            for stage in range(3):
                for copy in self.copies(stage, False):
                    copy.wait_send()


def chunks_of(widths):
    first, second = [], []
    for which, width in enumerate(widths):
        count = width // CHUNK
        later = max(1, round(count * 4 / 11))
        for i in range(count):
            (first if i < count - later else second).append((which, (i * CHUNK, CHUNK)))
    return first, second


def slots_of(first, second, stride=2):
    rows = []
    for slot in range(max(first, second) + 3 * stride):
        row = []
        for phase in (3, 2, 1, 0):
            if 0 <= slot - phase * stride < first:
                row.append((0, slot - phase * stride, phase))
            for chunk in range(second):
                if round(chunk * max(1, first) / max(1, second)) + phase * stride == slot:
                    row.append((1, chunk, phase))
        rows.append(row)
    return rows


class Gather:
    def __init__(self, shards, dims):
        self.dims, self.operands = dims, list(shards)
        self.widths = [shard.shape[1] for shard in shards]
        self.rows = shards[0].shape[0]
        self.plan = chunks_of(self.widths)
        self.count = sum(len(p) for p in self.plan)
        self.slots = slots_of(*(len(p) for p in self.plan))
        self.in_specs = [ANYWHERE] * len(shards)
        self.out_specs = [ANYWHERE] * len(shards)
        self.out_shape = [
            jax.ShapeDtypeStruct(dims + (self.rows, width), BF16) for width in self.widths
        ]
        most = max(dims) - 1
        self.scratch = [
            pltpu.SemaphoreType.DMA((self.count, 3, max(1, most))),
            pltpu.SemaphoreType.DMA((self.count, 3, max(1, most))),
            pltpu.SemaphoreType.DMA((self.count,)),
        ]

    def chunks(self, place, ins, outs, scratch):
        send, recv, local = scratch
        made, number = [], 0
        for order, plan in zip(GATHER_ORDERS, self.plan):
            group = []
            for which, columns in plan:
                group.append(
                    GatherChunk(
                        place,
                        ins[which],
                        outs[which],
                        columns,
                        order,
                        send.at[number],
                        recv.at[number],
                        local.at[number],
                    )
                )
                number += 1
            made.append(group)
        return made


class Scatter:
    def __init__(self, grads, dims):
        self.dims = dims
        total = dims[0] * dims[1] * dims[2]
        self.rows = grads[0].shape[0] // total
        self.widths = [grad.shape[1] for grad in grads]
        self.operands = [grad.reshape(dims + (self.rows, grad.shape[1])) for grad in grads]
        self.plan = chunks_of(self.widths)
        self.count = sum(len(p) for p in self.plan)
        self.slots = slots_of(*(len(p) for p in self.plan))
        self.in_specs = [ANYWHERE] * len(grads)
        self.out_specs = [pl.BlockSpec(memory_space=pltpu.VMEM)] * len(grads)
        self.out_shape = [jax.ShapeDtypeStruct((self.rows, width), F32) for width in self.widths]
        self.scratch = []
        for order, plan in zip(SCATTER_ORDERS, self.plan):
            c, b, a = order
            rest = tuple(dims[d] for d in range(3) if d != c)
            tile = (self.rows, CHUNK)
            held = max(1, len(plan))
            for lead in (
                rest,
                (max(1, dims[c] - 1),) + rest,
                (max(1, dims[b] - 1), dims[a]),
                (max(1, dims[a] - 1),),
            ):
                self.scratch.append(pltpu.VMEM((held,) + lead + tile, BF16))
        most = max(1, max(dims) - 1)
        self.scratch += [
            pltpu.SemaphoreType.DMA((self.count, 3, most)),
            pltpu.SemaphoreType.DMA((self.count, 3, most)),
            pltpu.SemaphoreType.DMA((self.count,)),
        ]

    def chunks(self, place, ins, outs, scratch):
        send, recv, local = scratch[8:]
        made, number = [], 0
        for side, (order, plan) in enumerate(zip(SCATTER_ORDERS, self.plan)):
            group = []
            for at, (which, columns) in enumerate(plan):
                group.append(
                    ScatterChunk(
                        place,
                        ins[which],
                        outs[which],
                        columns,
                        order,
                        [buffer.at[at] for buffer in scratch[4 * side : 4 * side + 4]],
                        send.at[number],
                        recv.at[number],
                        local.at[number],
                    )
                )
                number += 1
            made.append(group)
        return made


def transfer(plan, collective_id):
    def kernel(*refs):
        ins = refs[: len(plan.in_specs)]
        outs = refs[len(ins) : len(ins) + len(plan.out_specs)]
        place = Place(plan.dims)
        entry_barrier(place)
        groups = plan.chunks(place, ins, outs, refs[len(ins) + len(outs) :])
        for row in plan.slots:
            for order, chunk, phase in row:
                groups[order][chunk].act(phase)

    return pl.pallas_call(
        kernel,
        out_shape=plan.out_shape,
        in_specs=plan.in_specs,
        out_specs=plan.out_specs,
        scratch_shapes=plan.scratch,
        compiler_params=pltpu.CompilerParams(
            collective_id=collective_id, has_side_effects=True, vmem_limit_bytes=VMEM_BYTES
        ),
    )(*plan.operands)


def share_all(message, collective_id):
    dp, tensor = lax.axis_size("dp"), lax.axis_size("tensor")
    total = dp * tensor
    rows = message.shape[0]

    def kernel(message_ref, out_ref, held, send, recv):
        mine = lax.axis_index("dp") * tensor + lax.axis_index("tensor")

        def at(step):
            number = lax.rem(mine + step, total)
            return {"dp": number // tensor, "tensor": lax.rem(number, tensor)}

        barrier = pltpu.get_barrier_semaphore()

        def greet(step, carry):
            pl.semaphore_signal(barrier, inc=1, device_id=at(step), device_id_type=MESH_ID)
            return carry

        lax.fori_loop(1, total, greet, 0)
        pl.semaphore_wait(barrier, total - 1)

        def copy(step, slot):
            return pltpu.make_async_remote_copy(
                src_ref=message_ref,
                dst_ref=held.at[slot],
                send_sem=send.at[step],
                recv_sem=recv.at[step],
                device_id=at(step),
                device_id_type=MESH_ID,
            )

        def start(step, carry):
            copy(step, mine).start()
            return carry

        lax.fori_loop(1, total, start, 0)
        held[mine] = message_ref[...]

        def finish(step, carry):
            copy(step, lax.rem(mine + total - step, total)).wait_recv()
            return carry

        lax.fori_loop(1, total, finish, 0)

        def sent(step, carry):
            copy(step, mine).wait_send()
            return carry

        lax.fori_loop(1, total, sent, 0)
        out_ref[...] = held[...]

    out = pl.pallas_call(
        kernel,
        out_shape=jax.ShapeDtypeStruct((total, rows, 128), F32),
        in_specs=[pl.BlockSpec(memory_space=pltpu.VMEM)],
        out_specs=pl.BlockSpec(memory_space=pltpu.VMEM),
        scratch_shapes=[
            pltpu.VMEM((total, rows, 128), F32),
            pltpu.SemaphoreType.DMA((total,)),
            pltpu.SemaphoreType.DMA((total,)),
        ],
        compiler_params=pltpu.CompilerParams(collective_id=collective_id, has_side_effects=True),
    )(message)
    return out.reshape(dp, tensor, rows, 128)


def rotary_tables():
    half_size = HEAD_WIDTH // 2
    frequency = jnp.power(
        theta_base, -2.0 * jnp.arange(half_size, dtype=F32) / HEAD_WIDTH
    )
    angles = frequency[:, None] * jnp.arange(SEQUENCE_LENGTH, dtype=F32)[None, :]
    return jnp.cos(angles), jnp.sin(angles)


def rotate(values, cosine, sine, sign):
    half = HEAD_WIDTH // 2
    top, bottom = values[:half], values[half:]
    return jnp.concatenate(
        [top * cosine - sign * (bottom * sine), bottom * cosine + sign * (top * sine)], 0
    )


def product(left, right, left_dim=1, right_dim=0):
    return lax.dot_general(
        left, right, (((left_dim,), (right_dim,)), ((), ())), preferred_element_type=F32
    )


def row_scale(values):
    return lax.rsqrt(jnp.mean(values * values, -1, keepdims=True) + norm_eps)


def compute_call(kernel, name, **kwargs):
    return pl.pallas_call(
        kernel,
        name=name,
        compiler_params=pltpu.CompilerParams(vmem_limit_bytes=VMEM_BYTES),
        **kwargs,
    )


def project(rows, gain, weights, cosine, sine):
    tokens, width = rows.shape
    features = weights.shape[1]
    block = 512
    turned = features * 3 // 4

    def kernel(x_ref, gain_ref, w_ref, cos_ref, sin_ref, n_ref, out_ref):
        x = x_ref[...].astype(F32)
        normed = (x * row_scale(x) * gain_ref[...]).astype(BF16)
        n_ref[...] = normed
        raw = product(w_ref[...], normed, 0, 1)
        cosine, sine = cos_ref[...], sin_ref[...]
        for first in range(0, turned, HEAD_WIDTH):
            rows = slice(first, first + HEAD_WIDTH)
            out_ref[rows] = rotate(raw[rows], cosine, sine, 1.0).astype(BF16)
        out_ref[turned:] = raw[turned:].astype(BF16)

    per_sequence = SEQUENCE_LENGTH // block
    table = pl.BlockSpec((HEAD_WIDTH // 2, block), lambda i: (0, lax.rem(i, per_sequence)))
    return compute_call(
        kernel,
        "project",
        grid=(tokens // block,),
        in_specs=[
            pl.BlockSpec((block, width), lambda i: (i, 0)),
            pl.BlockSpec((1, width), lambda i: (0, 0)),
            pl.BlockSpec((width, features), lambda i: (0, 0)),
            table,
            table,
        ],
        out_specs=[
            pl.BlockSpec((block, width), lambda i: (i, 0)),
            pl.BlockSpec((features, block), lambda i: (0, i)),
        ],
        out_shape=[
            jax.ShapeDtypeStruct((tokens, width), BF16),
            jax.ShapeDtypeStruct((features, tokens), BF16),
        ],
    )(rows, gain, weights, cosine, sine)


def visible(prefix, first):
    place = lax.broadcasted_iota(jnp.int32, (1, QUERY_CHUNK), 1) + first
    limit = jnp.maximum(place + 1, prefix)
    return lax.broadcasted_iota(jnp.int32, (SEQUENCE_LENGTH, QUERY_CHUNK), 0) < limit


def attention_specs(features):
    kv_heads = features // HEAD_WIDTH // (GROUP_WIDTH + 2)
    q_heads = kv_heads * GROUP_WIDTH
    wide = (GROUP_WIDTH * HEAD_WIDTH, SEQUENCE_LENGTH)
    slim = (HEAD_WIDTH, SEQUENCE_LENGTH)
    query = pl.BlockSpec(wide, lambda s, j, p: (j, s))
    key = pl.BlockSpec(slim, lambda s, j, p: (q_heads + j, s))
    value = pl.BlockSpec(slim, lambda s, j, p: (q_heads + kv_heads + j, s))
    sums = pl.BlockSpec((None, GROUP_WIDTH, SEQUENCE_LENGTH), lambda s, j, p: (j, 0, s))
    return kv_heads, q_heads, query, key, value, sums


def attend_forward(qkv, prefixes):
    features, tokens = qkv.shape
    kv_heads, q_heads, query, key, value, sums = attention_specs(features)
    scale = SCORE_SCALE * LOG2_E

    def kernel(prefix_ref, q_ref, k_ref, v_ref, mixed_ref, sum_ref):
        prefix = prefix_ref[pl.program_id(0)]
        keys = k_ref[...].T
        values = jnp.concatenate([v_ref[...], jnp.ones((16, SEQUENCE_LENGTH), BF16)], 0)
        for head in range(GROUP_WIDTH):
            rows = slice(head * HEAD_WIDTH, (head + 1) * HEAD_WIDTH)
            for first in range(0, SEQUENCE_LENGTH, QUERY_CHUNK):
                columns = slice(first, first + QUERY_CHUNK)
                scores = product(keys, q_ref[rows, columns])
                scores = jnp.where(visible(prefix, first), scores, neg_fill)
                peak = jnp.max(scores, 0, keepdims=True) * scale
                weights = jnp.exp2(scores * scale - peak).astype(BF16)
                out = product(values, weights)
                total = out[HEAD_WIDTH : HEAD_WIDTH + 1]
                mixed_ref[rows, columns] = (out[:HEAD_WIDTH] * (1.0 / total)).astype(BF16)
                sum_ref[head : head + 1, columns] = peak + jnp.log2(total)

    return compute_call(
        kernel,
        "attend_forward",
        grid_spec=pltpu.PrefetchScalarGridSpec(
            num_scalar_prefetch=1,
            grid=(tokens // SEQUENCE_LENGTH, kv_heads),
            in_specs=[query, key, value],
            out_specs=[query, sums],
        ),
        out_shape=[
            jax.ShapeDtypeStruct((q_heads * HEAD_WIDTH, tokens), BF16),
            jax.ShapeDtypeStruct((kv_heads, GROUP_WIDTH, tokens), F32),
        ],
    )(prefixes, qkv, qkv, qkv)


def attend_backward(qkv, dmixed, mixed, logsums, prefixes, cosine, sine):
    features, tokens = qkv.shape
    kv_heads, q_heads, query, key, value, sums = attention_specs(features)
    scale = SCORE_SCALE * LOG2_E

    def kernel(
        prefix_ref,
        q_ref,
        k_ref,
        v_ref,
        d_ref,
        mixed_ref,
        sum_ref,
        cos_ref,
        sin_ref,
        dq_ref,
        dk_ref,
        dv_ref,
    ):
        prefix = prefix_ref[pl.program_id(0)]
        keys_flat = k_ref[...]
        keys, values = keys_flat.T, v_ref[...].T
        dkeys = jnp.zeros((SEQUENCE_LENGTH, HEAD_WIDTH), F32)
        dvalues = jnp.zeros((SEQUENCE_LENGTH, HEAD_WIDTH), F32)
        cosine, sine = cos_ref[...], sin_ref[...]
        for head in range(GROUP_WIDTH):
            rows = slice(head * HEAD_WIDTH, (head + 1) * HEAD_WIDTH)
            for first in range(0, SEQUENCE_LENGTH, QUERY_CHUNK):
                columns = slice(first, first + QUERY_CHUNK)
                q, d = q_ref[rows, columns], d_ref[rows, columns]
                delta = jnp.sum(
                    d.astype(F32) * mixed_ref[rows, columns].astype(F32), 0, keepdims=True
                )
                scores = product(keys, q) * scale
                weights = jnp.exp2(scores - sum_ref[head : head + 1, columns])
                weights = jnp.where(visible(prefix, first), weights, 0.0)
                dweights = product(values, d)
                dscores = (weights * (dweights - delta)).astype(BF16)
                dvalues = dvalues + product(weights.astype(BF16), d.T)
                dkeys = dkeys + product(dscores, q.T)
                dq = product(keys_flat, dscores) * SCORE_SCALE
                dq_ref[rows, columns] = rotate(
                    dq, cosine[:, columns], sine[:, columns], -1.0
                ).astype(BF16)
        dk_ref[...] = rotate((dkeys * SCORE_SCALE).T, cosine, sine, -1.0).astype(BF16)
        dv_ref[...] = dvalues.T.astype(BF16)

    slim = pl.BlockSpec((HEAD_WIDTH, SEQUENCE_LENGTH), lambda s, j, p: (j, s))
    table = pl.BlockSpec((HEAD_WIDTH // 2, SEQUENCE_LENGTH), lambda s, j, p: (0, 0))
    return compute_call(
        kernel,
        "attend_backward",
        grid_spec=pltpu.PrefetchScalarGridSpec(
            num_scalar_prefetch=1,
            grid=(tokens // SEQUENCE_LENGTH, kv_heads),
            in_specs=[query, key, value, query, query, sums, table, table],
            out_specs=[query, slim, slim],
        ),
        out_shape=[
            jax.ShapeDtypeStruct((q_heads * HEAD_WIDTH, tokens), BF16),
            jax.ShapeDtypeStruct((kv_heads * HEAD_WIDTH, tokens), BF16),
            jax.ShapeDtypeStruct((kv_heads * HEAD_WIDTH, tokens), BF16),
        ],
    )(prefixes, qkv, qkv, qkv, dmixed, mixed, logsums, cosine, sine)


def feed_forward(rows, gate_full, up_full):
    tokens, width = rows.shape
    units = gate_full.shape[1]
    tall, wide = 1024, 512

    def kernel(n_ref, gate_w, up_w, gate_ref, up_ref, hidden_ref):
        normed = n_ref[...]
        gate = product(normed, gate_w[...])
        up = product(normed, up_w[...])
        gate_ref[...] = gate.astype(BF16)
        up_ref[...] = up.astype(BF16)
        hidden_ref[...] = (gate * jax.nn.sigmoid(gate) * up).astype(BF16)

    weight = pl.BlockSpec((width, wide), lambda i, j: (0, j))
    out = pl.BlockSpec((tall, wide), lambda i, j: (i, j))
    return compute_call(
        kernel,
        "feed_forward",
        grid=(tokens // tall, units // wide),
        in_specs=[pl.BlockSpec((tall, width), lambda i, j: (i, 0)), weight, weight],
        out_specs=[out, out, out],
        out_shape=[jax.ShapeDtypeStruct((tokens, units), BF16)] * 3,
    )(rows, gate_full, up_full)


def feed_backward(back_rows, down_full, gate, up):
    tokens, width = back_rows.shape
    units = down_full.shape[1]
    tall, wide = 1024, 512

    def kernel(d_ref, down_w, gate_ref, up_ref, dgate_ref, dup_ref):
        dhidden = product(d_ref[...], down_w[...])
        gate = gate_ref[...].astype(F32)
        sigmoid = jax.nn.sigmoid(gate)
        dup_ref[...] = (dhidden * gate * sigmoid).astype(BF16)
        dgate_ref[...] = (
            dhidden * up_ref[...].astype(F32) * sigmoid * (1.0 + gate * (1.0 - sigmoid))
        ).astype(BF16)

    tile = pl.BlockSpec((tall, wide), lambda i, j: (i, j))
    return compute_call(
        kernel,
        "feed_backward",
        grid=(tokens // tall, units // wide),
        in_specs=[
            pl.BlockSpec((tall, width), lambda i, j: (i, 0)),
            pl.BlockSpec((width, wide), lambda i, j: (0, j)),
            tile,
            tile,
        ],
        out_specs=[tile, tile],
        out_shape=[jax.ShapeDtypeStruct((tokens, units), BF16)] * 2,
    )(back_rows, down_full, gate, up)


def second_norm_grad(dgate, dup, gate_full, up_full):
    tokens, units = dgate.shape
    width = gate_full.shape[0]
    block = 256

    def kernel(dgate_ref, dup_ref, gate_w, up_w, out_ref):
        out_ref[...] = (
            product(dgate_ref[...], gate_w[...], 1, 1) + product(dup_ref[...], up_w[...], 1, 1)
        ).astype(BF16)

    rows = pl.BlockSpec((block, units), lambda i: (i, 0))
    weight = pl.BlockSpec((width, units), lambda i: (0, 0), pipeline_mode=pl.Buffered(1))
    return compute_call(
        kernel,
        "second_norm_grad",
        grid=(tokens // block,),
        in_specs=[rows, rows, weight, weight],
        out_specs=pl.BlockSpec((block, width), lambda i: (i, 0)),
        out_shape=jax.ShapeDtypeStruct((tokens, width), BF16),
    )(dgate, dup, gate_full, up_full)


def tensor_sum(partial):
    other = lax.ppermute(partial, "tensor", [(0, 1), (1, 0)])
    return partial.astype(F32) + other.astype(F32)


def norm_back(dnorm, gain_row, unit_rows, inverse):
    scaled = dnorm * gain_row
    return inverse * (scaled - unit_rows * jnp.mean(scaled * unit_rows, -1, keepdims=True))


def adam_step(weight, gradient, first_moment, second_moment, rate, decay, factor, fix_one, fix_two):
    clipped = factor * gradient
    first_new = beta_one * first_moment + (1.0 - beta_one) * clipped
    second_new = beta_two * second_moment + (1.0 - beta_two) * clipped * clipped
    update = first_new / fix_one / (jnp.sqrt(second_new / fix_two) + adam_eps) + decay * weight
    return (weight - rate * update, first_new, second_new)


def local(
    block_in,
    prefix_len,
    out_grad,
    step_count,
    q_weight,
    key_matrix,
    value_matrix,
    o_weight,
    gate_weight,
    up_weight,
    down_weight,
    norm_gains,
    query_mean_moment,
    key_mean_moment,
    value_mean_moment,
    output_mean_moment,
    gate_mean_moment,
    up_mean_moment,
    down_mean_moment,
    gains_mean_moment,
    q_second,
    key_square_moment,
    value_square_moment,
    o_second,
    gate_second,
    up_second,
    down_second,
    gains_second,
):
    dims = factor(lax.axis_size("dp"))
    width = block_in.shape[1]
    q_width, kv_width = q_weight.shape[1], key_matrix.shape[1]
    units = gate_weight.shape[1]
    qkv_low = jnp.concatenate([q_weight, key_matrix, value_matrix], 1).astype(BF16)
    (qkv_full,) = transfer(Gather([qkv_low], dims), 0)
    o_full, gate_full, up_full, down_full = transfer(
        Gather([w.astype(BF16) for w in (o_weight, gate_weight, up_weight, down_weight)], dims), 1
    )
    qkv_full = qkv_full.reshape(width, -1)
    o_full = o_full.reshape(width, -1)
    gate_full, up_full, down_full = (
        w.reshape(width, units) for w in (gate_full, up_full, down_full)
    )
    cosine, sine = rotary_tables()

    normed_one, qkv = project(block_in, norm_gains[:1], qkv_full, cosine, sine)
    mixed, logsums = attend_forward(qkv, prefix_len)
    input_rows = block_in.astype(F32)
    middle = input_rows + tensor_sum(product(mixed, o_full, 0, 1).astype(BF16))
    inverse_two = row_scale(middle)
    normed_two = (middle * inverse_two * norm_gains[1]).astype(BF16)
    gate, up, hidden = feed_forward(normed_two, gate_full, up_full)

    grad_down = product(out_grad, hidden, 0, 0).astype(BF16)
    block_out = (middle + tensor_sum(product(hidden, down_full, 1, 1).astype(BF16))).astype(BF16)
    dgate, dup = feed_backward(out_grad, down_full, gate, up)
    grad_gate = product(normed_two, dgate, 0, 0).astype(BF16)
    grad_up = product(normed_two, dup, 0, 0).astype(BF16)
    dnorm_two = tensor_sum(second_norm_grad(dgate, dup, gate_full, up_full))
    unit_two = middle * inverse_two
    gain_two = jnp.sum(dnorm_two * unit_two, 0)
    dmiddle = out_grad.astype(F32) + norm_back(dnorm_two, norm_gains[1], unit_two, inverse_two)
    dmiddle_low = dmiddle.astype(BF16)
    grad_out = product(dmiddle_low, mixed, 0, 1).astype(BF16)
    dmixed = product(o_full, dmiddle_low, 0, 1).astype(BF16)
    dquery, dkey, dvalue = attend_backward(
        qkv, dmixed, mixed, logsums, prefix_len, cosine, sine
    )
    dqkv = jnp.concatenate([dquery, dkey, dvalue], 0)
    grad_qkv = product(normed_one, dqkv, 0, 1).astype(BF16)
    dnorm_one = tensor_sum(product(dqkv, qkv_full, 0, 1).astype(BF16))
    inverse_one = row_scale(input_rows)
    unit_one = input_rows * inverse_one
    gain_one = jnp.sum(dnorm_one * unit_one, 0)
    in_grad = dmiddle + norm_back(dnorm_one, norm_gains[0], unit_one, inverse_one)

    sum_qkv, sum_out, sum_gate, sum_up, sum_down = transfer(
        Scatter([grad_qkv, grad_out, grad_gate, grad_up, grad_down], dims), 2
    )
    shares = (sum_qkv, sum_out, sum_gate, sum_up, sum_down)
    squares = sum(jnp.sum(jnp.square(share)) for share in shares)
    gain_rows = 2 * width // 128
    message = jnp.concatenate(
        [
            jnp.stack([gain_one, gain_two]).reshape(gain_rows, 128),
            jnp.broadcast_to(squares, (8, 128)),
        ],
        0,
    )
    everyone = share_all(message, 3)
    gain_sum = jnp.sum(everyone[:, 0, :gain_rows], 0)
    total_square = jnp.sum(everyone[:, :, gain_rows, 0]) + jnp.sum(jnp.square(gain_sum))
    gain_width = width // lax.axis_size("dp")
    first_column = lax.axis_index("dp") * gain_width
    grad_gains = lax.dynamic_slice_in_dim(gain_sum.reshape(2, width), first_column, gain_width, 1)
    old_gains = lax.dynamic_slice_in_dim(norm_gains, first_column, gain_width, 1)
    reduced = (
        sum_qkv[:, :q_width],
        sum_qkv[:, q_width : q_width + kv_width],
        sum_qkv[:, q_width + kv_width :],
        sum_out,
        sum_gate,
        sum_up,
        sum_down,
        grad_gains,
    )
    grad_norm = jnp.sqrt(total_square)
    factor_now = jnp.minimum(1.0, clip_limit / grad_norm)
    step_float = step_count[0].astype(F32)
    fix_one = 1.0 - jnp.power(beta_one, step_float)
    fix_two = 1.0 - jnp.power(beta_two, step_float)
    masters = (
        q_weight,
        key_matrix,
        value_matrix,
        o_weight,
        gate_weight,
        up_weight,
        down_weight,
        old_gains,
    )
    firsts = (
        query_mean_moment,
        key_mean_moment,
        value_mean_moment,
        output_mean_moment,
        gate_mean_moment,
        up_mean_moment,
        down_mean_moment,
        gains_mean_moment,
    )
    seconds = (
        q_second,
        key_square_moment,
        value_square_moment,
        o_second,
        gate_second,
        up_second,
        down_second,
        gains_second,
    )
    rate_list = matrix_rates + (gain_rate,)
    decay_list = (decay_rate,) * 7 + (0.0,)
    new_weights, new_firsts, new_seconds = ([], [], [])
    for weight, gradient, first_moment, second_moment, rate, decay in zip(
        masters, reduced, firsts, seconds, rate_list, decay_list
    ):
        weight_new, first_new, second_new = adam_step(
            weight, gradient, first_moment, second_moment, rate, decay, factor_now, fix_one, fix_two
        )
        new_weights.append(weight_new)
        new_firsts.append(first_new)
        new_seconds.append(second_new)
    return (
        block_out,
        in_grad,
        grad_norm.reshape(1),
        new_weights[0],
        new_weights[1],
        new_weights[2],
        new_weights[3],
        new_weights[4],
        new_weights[5],
        new_weights[6],
        new_weights[7],
        new_firsts[0],
        new_firsts[1],
        new_firsts[2],
        new_firsts[3],
        new_firsts[4],
        new_firsts[5],
        new_firsts[6],
        new_firsts[7],
        new_seconds[0],
        new_seconds[1],
        new_seconds[2],
        new_seconds[3],
        new_seconds[4],
        new_seconds[5],
        new_seconds[6],
        new_seconds[7],
    )


def solution(mesh):
    return jax.shard_map(
        local,
        mesh=mesh,
        in_specs=(
            P("dp", None),
            P("dp"),
            P("dp", None),
            P(),
            P("dp", "tensor"),
            P("dp", "tensor"),
            P("dp", "tensor"),
            P("dp", "tensor"),
            P("dp", "tensor"),
            P("dp", "tensor"),
            P("dp", "tensor"),
            P(),
            P("dp", "tensor"),
            P("dp", "tensor"),
            P("dp", "tensor"),
            P("dp", "tensor"),
            P("dp", "tensor"),
            P("dp", "tensor"),
            P("dp", "tensor"),
            P(None, "dp"),
            P("dp", "tensor"),
            P("dp", "tensor"),
            P("dp", "tensor"),
            P("dp", "tensor"),
            P("dp", "tensor"),
            P("dp", "tensor"),
            P("dp", "tensor"),
            P(None, "dp"),
        ),
        out_specs=(
            P("dp", None),
            P("dp", None),
            P(),
            P("dp", "tensor"),
            P("dp", "tensor"),
            P("dp", "tensor"),
            P("dp", "tensor"),
            P("dp", "tensor"),
            P("dp", "tensor"),
            P("dp", "tensor"),
            P(None, "dp"),
            P("dp", "tensor"),
            P("dp", "tensor"),
            P("dp", "tensor"),
            P("dp", "tensor"),
            P("dp", "tensor"),
            P("dp", "tensor"),
            P("dp", "tensor"),
            P(None, "dp"),
            P("dp", "tensor"),
            P("dp", "tensor"),
            P("dp", "tensor"),
            P("dp", "tensor"),
            P("dp", "tensor"),
            P("dp", "tensor"),
            P("dp", "tensor"),
            P(None, "dp"),
        ),
        check_vma=False,
    )
```

time: 2600 us -> 960 us (0.37)
  waiting for transfers between devices: 1610 us -> 9.77 us
  Pallas kernels: 0 us -> 681 us
  matrix products: 514 us -> 130 us
  local copies, waits for them, and re-layouts: 182 us -> 8.54 us
  other arithmetic: 201 us -> 110 us
  blocking collectives: 40.4 us -> 0 us
    reduce_scatter x7 -> x0, waiting for transfers between devices: 1090 us -> none  [the longest x1 207 us: local(): lax.psum_scatter(grad_up, 'dp', scatter_dimension=0, tiled=True)]
    pallas_call x0 -> x10, Pallas kernels: none -> 681 us  [the longest x3 468 us: transfer(): pl.pallas_call(kernel, out_shape=plan.out_shape, in_specs=plan.in_specs,...]
    all_gather x7 -> x0, waiting for transfers between devices: 394 us -> none  [the longest x1 87.1 us: local(): lax.all_gather(gate_low, 'dp', axis=0, tiled=True)]
    dot_general x70 -> x9, matrix products: 514 us -> 130 us  [product(): lax.dot_general(left, right, (((left_dim,), (right_dim,)), ((), ())), pre...]
    dynamic_update_slice x8 -> x0, local copies, waits for them, and re-layouts: 122 us -> none  [attend_forward(): return lax.map(one_block, jnp.arange(block_list, dtype=jnp.int32))]
    unnamed x19 -> x0, waiting for transfers between devices: 93.3 us -> none
    convert_element_type x18 -> x5, other arithmetic: 66.2 us -> 15.7 us  [the longest x1 8.32 us: local(): normed_two = (middle * inverse_two * norm_gains[1]).astype(BF16)]
    psum x1 -> x0, blocking collectives: 40.4 us -> none  [local(): total_square = lax.psum(squares, ('dp', 'tensor'))]
  transfers between devices with their start and end apart: 18 -> 4, of which waited for: 16 -> 1; matrix products, arithmetic and copies ran while one was open for 14% -> 12% of each run, Pallas kernels for 0% -> 23%
where the time goes in v1:
time: 960 us; the launch traced here: 948 us
  Pallas kernels  681 us (71%)
  matrix products  130 us (14%)
  other arithmetic  110 us (11%)
  waiting for transfers between devices  9.77 us (1%)
    pallas_call x3, Pallas kernels, transfer(): pl.pallas_call(kernel, out_shape=plan.out_shape, in_specs=plan.in_specs,...  468 us
    dot_general x9, matrix products, product(): lax.dot_general(left, right, (((left_dim,), (right_dim,)), ((), ())), pre...  130 us
    pallas_call x1, Pallas kernels, attend_backward(): compute_call(kernel, 'attend_backward', grid_spec=pltpu.PrefetchScalarGri...  51.4 us
    pallas_call x1, Pallas kernels, attend_forward(): compute_call(kernel, 'attend_forward', grid_spec=pltpu.PrefetchScalarGrid...  35.6 us
    pallas_call x1, Pallas kernels, second_norm_grad(): compute_call(kernel, 'second_norm_grad', grid=(tokens // block,), in_spec...  33.8 us
    pallas_call x1, Pallas kernels, feed_forward(): compute_call(kernel, 'feed_forward', grid=(tokens // tall, units // wide)...  32.6 us
    pallas_call x1, Pallas kernels, feed_backward(): compute_call(kernel, 'feed_backward', grid=(tokens // tall, units // wide...  26.4 us
    add x1, other arithmetic, local(): out_grad.astype(F32)  20.6 us
  transfers between devices with their start and end apart: 4, of which 1 were waited for; matrix products, arithmetic and copies ran while one was open for 12% of the time, Pallas kernels for 23%

profile of v1, /device:TPU:0, one launch (start us, length us, event | category | flops | bytes accessed | tf_op | source)
XLA Modules:
  0.0 947.7 jit_solution(11908317036811507866)
XLA Ops:
  0.7 2.0 slice_reduce_fusion.3
  3.6 0.9 convert.11
  4.5 1.0 convert.9
  5.5 1.6 convert_element_type.87.refs_0_
  7.1 1.5 fusion.18
  8.7 1.9 convert_element_type.88.refs_1_
  10.6 1.9 convert_element_type.89.refs_2_
  12.5 1.9 convert_element_type.90.refs_3_
  15.2 60.4 %shard_map.475 = bf16[4,2,2,96,1536]{4,3,2,1,0:T(8,128)(2,1)} custom-call(bf16[96,1536]{1,0:T(8,128)(2,1)} %pad_maximum_fusion.refs_0_), custom_call_target="tpu_custom_call" | custom-call | tf_op jit(solution)/shard_map/pallas_call | solution.py:351
  75.6 17.3 %project.1 = (bf16[2048,1536]{1,0:T(8,128)(2,1)}, bf16[1536,2048]{1,0:T(8,128)(2,1)}) custom-call(bf16[2048,1536]{1,0:T(8,128)(2,1)} %x_ref.1, f32[1,1536]{1,0:T(1,128)} %get-tuple-element.107.gain_ref, bf16[1536,1536]{1,0:T(8,128)(2,1)} %bitcast.46, f32[48,1024]{1,0:T(8,128)} %get-tuple-element.109.cos_ref, f32[48,1024]{1,0:T(8,128)} %get-tuple-element.108.sin_ref), custom_call_target="tpu_custom_call" | custom-call | tf_op jit(solution)/shard_map/project/pallas_call | solution.py:484
  92.9 35.6 %attend_forward.1 = (bf16[768,2048]{1,0:T(8,128)(2,1)}, f32[4,2,2048]{2,1,0:T(2,128)}) custom-call(s32[2]{0:T(128)} %prefix_ref.3, bf16[1536,2048]{1,0:T(8,128)(2,1)} %get-tuple-element.48.q_ref.k_ref.v_ref, bf16[1536,2048]{1,0:T(8,128)(2,1)} %get-tuple-element.48.q_ref.k_ref.v_ref, bf16[1536,2048]{1,0:T(8,128)(2,1)} %get-tuple-element.48.q_ref.k_ref.v_ref), custom_call_target="tpu_custom_call" | custom-call | tf_op jit(solution)/shard_map/attend_forward/pallas_call | solution.py:546
  128.5 185.5 %shard_map.476 = (bf16[4,2,2,96,768]{4,3,2,1,0:T(8,128)(2,1)}, bf16[4,2,2,96,2048]{4,3,2,1,0:T(8,128)(2,1)}, bf16[4,2,2,96,2048]{4,3,2,1,0:T(8,128)(2,1)}, bf16[4,2,2,96,2048]{4,3,2,1,0:T(8,128)(2,1)}) custom-call(bf16[96,768]{1,0:T(8,128)(2,1)} %convert_element_type.87.refs_0_, bf16[96,2048]{1,0:T(8,128)(2,1)} %convert_element_type.88.refs_1_, ...), custom_call_target="tpu_custom_call" | custom-call | tf_op jit(solution)/shard_map/pallas_call | solution.py:351
  314.0 9.2 convolution_convert_fusion
  323.9 9.8 %collective-permute-done = bf16[2048,1536]{1,0:T(8,128)(2,1)} collective-permute-done((bf16[2048,1536]{1,0:T(8,128)(2,1)}, bf16[2048,1536]{1,0:T(8,128)(2,1)}, u32[]{:S(2)}, u32[]{:S(2)}) %collective-permute-start) | collective-permute-done | bytes 6291488 | tf_op jit(solution)/shard_map/ppermute | solution.py:706
  333.6 13.0 %multiply_reduce_fusion.2 = (f32[2048]{0:T(1024)S(1)}, f32[2048,1536]{1,0:T(8,128)}, f32[2048]{0:T(1024)S(1)}) fusion(bf16[2048,1536]{1,0:T(8,128)(2,1)} %collective-permute-done, bf16[2048,1536]{1,0:T(8,128)(2,1)} %convolution_convert_fusion, bf16[2048,1536]{1,0:T(8,128)(2,1)} %x_ref.1), kind=kLoop, calls=%fused_computation.19 | loop fusion | flops 28307456 | bytes 31473664 | tf_op jit(solution)/shard_map/reduce_sum | solution.py:453
  346.6 8.3 multiply_convert_fusion.n_ref
  354.9 32.6 %feed_forward.1 = (bf16[2048,2048]{1,0:T(8,128)(2,1)}, bf16[2048,2048]{1,0:T(8,128)(2,1)}, bf16[2048,2048]{1,0:T(8,128)(2,1)}) custom-call(bf16[2048,1536]{1,0:T(8,128)(2,1)} %multiply_convert_fusion.n_ref, bf16[1536,2048]{1,0:T(8,128)(2,1)} %bitcast.42, bf16[1536,2048]{1,0:T(8,128)(2,1)} %bitcast.44), custom_call_target="tpu_custom_call" | custom-call | tf_op jit(solution)/shard_map/feed_forward/pallas_call | solution.py:643
  387.5 26.4 %feed_backward.1 = (bf16[2048,2048]{1,0:T(8,128)(2,1)}, bf16[2048,2048]{1,0:T(8,128)(2,1)}) custom-call(bf16[2048,1536]{1,0:T(8,128)(2,1)} %d_ref.1, bf16[1536,2048]{1,0:T(8,128)(2,1)} %bitcast.48, bf16[2048,2048]{1,0:T(8,128)(2,1)} %get-tuple-element.55.gate_ref, bf16[2048,2048]{1,0:T(8,128)(2,1)} %get-tuple-element.56.up_ref), custom_call_target="tpu_custom_call" | custom-call | tf_op jit(solution)/shard_map/feed_backward/pallas_call | solution.py:668
  413.8 33.8 %second_norm_grad.1 = bf16[2048,1536]{1,0:T(8,128)(2,1)} custom-call(bf16[2048,2048]{1,0:T(8,128)(2,1)} %get-tuple-element.57.dgate_ref, bf16[2048,2048]{1,0:T(8,128)(2,1)} %get-tuple-element.58.dup_ref, bf16[1536,2048]{1,0:T(8,128)(2,1)} %bitcast.43, bf16[1536,2048]{1,0:T(8,128)(2,1)} %bitcast.45), custom_call_target="tpu_custom_call" | custom-call | tf_op jit(solution)/shard_map/second_norm_grad/pallas_call | solution.py:695
  447.8 19.2 %convolution_convert_fusion.2 = bf16[2048,1536]{1,0:T(8,128)(2,1)} fusion(bf16[2048,2048]{1,0:T(8,128)(2,1)} %get-tuple-element.53, bf16[1536,2048]{1,0:T(8,128)(2,1)} %bitcast.49), kind=kOutput, calls=%fused_computation.24 | convolution fusion | flops 12888047616 | bytes 20971520 | tf_op jit(solution)/shard_map/dot_general | solution.py:447
  468.0 19.2 %convolution_convert_fusion.4 = bf16[1536,2048]{1,0:T(8,128)(2,1)} fusion(bf16[2048,1536]{1,0:T(8,128)(2,1)} %multiply_convert_fusion.n_ref, bf16[2048,2048]{1,0:T(8,128)(2,1)} %get-tuple-element.58.dup_ref), kind=kOutput, calls=%fused_computation.26 | convolution fusion | flops 12888047616 | bytes 20971520 | tf_op jit(solution)/shard_map/dot_general | solution.py:447
  487.2 19.5 %convolution_convert_fusion.3 = bf16[2048,1536]{0,1:T(8,128)(2,1)} fusion(bf16[2048,2048]{1,0:T(8,128)(2,1)} %get-tuple-element.53, bf16[2048,1536]{1,0:T(8,128)(2,1)} %d_ref.1), kind=kOutput, calls=%fused_computation.25 | convolution fusion | flops 12888047616 | bytes 20971520 | tf_op jit(solution)/shard_map/dot_general | solution.py:447
  506.8 5.2 multiply_reduce_fusion
  512.0 20.6 %multiply_add_fusion = (f32[2048,1536]{1,0:T(8,128)}, bf16[2048,1536]{1,0:T(8,128)(2,1)}) fusion(bf16[2048,1536]{1,0:T(8,128)(2,1)} %d_ref.1, bf16[2048,1536]{1,0:T(8,128)(2,1)} %copy-done, bf16[2048,1536]{1,0:T(8,128)(2,1)} %second_norm_grad.1, f32[2048,1536]{1,0:T(8,128)S(1)} %bitcast.33, f32[2048]{0:T(1024)S(1)} %broadcast_multiply_fusion.1, ...), kind=kLoop, calls=%fused_computation.14 | loop fusion | flops 47185920 | bytes 62937088 | tf_op jit(solution)/shard_map/add | solution.py:785
  532.6 10.0 %convolution_convert_fusion.8.d_ref = bf16[768,2048]{1,0:T(8,128)(2,1)} fusion(bf16[1536,768]{1,0:T(8,128)(2,1)} %bitcast.58, f32[2048,1536]{1,0:T(8,128)} %get-tuple-element.101), kind=kOutput, calls=%fused_computation.30 | convolution fusion | flops 4836556800 | bytes 18087936 | tf_op jit(solution)/shard_map/dot_general | solution.py:447
  542.6 51.4 %attend_backward.1 = (bf16[768,2048]{1,0:T(8,128)(2,1)}, bf16[384,2048]{1,0:T(8,128)(2,1)}, bf16[384,2048]{1,0:T(8,128)(2,1)}) custom-call(s32[2]{0:T(128)} %prefix_ref.3, bf16[1536,2048]{1,0:T(8,128)(2,1)} %get-tuple-element.48.q_ref.k_ref.v_ref, bf16[1536,2048]{1,0:T(8,128)(2,1)} %get-tuple-element.48.q_ref.k_ref.v_ref, ...), custom_call_target="tpu_custom_call" | custom-call | tf_op jit(solution)/shard_map/attend_backward/pallas_call | solution.py:611
  594.1 2.3 constant_dynamic-update-slice_fusion.2
  597.1 2.8 copy-done.8
  599.8 14.4 %convolution_convert_fusion.1 = bf16[2048,1536]{1,0:T(8,128)(2,1)} fusion(bf16[1536,2048]{1,0:T(8,128)(2,1)S(1)} %constant_dynamic-update-slice_fusion, bf16[1536,1536]{1,0:T(8,128)(2,1)} %bitcast.47), kind=kOutput, calls=%fused_computation.23 | convolution fusion | flops 9666822144 | bytes 17301504 | tf_op jit(solution)/shard_map/dot_general | solution.py:447
  614.4 18.7 %convolution_convert_fusion.5 = bf16[1536,2048]{1,0:T(8,128)(2,1)} fusion(bf16[2048,1536]{1,0:T(8,128)(2,1)S(1)} %bitcast.41, bf16[2048,2048]{1,0:T(8,128)(2,1)} %get-tuple-element.57.dgate_ref), kind=kOutput, calls=%fused_computation.27 | convolution fusion | flops 12888047616 | bytes 20971520 | tf_op jit(solution)/shard_map/dot_general | solution.py:447
  633.1 6.6 convolution_convert_fusion.7
  639.7 13.7 %convolution_convert_fusion.6 = bf16[1536,1536]{1,0:T(8,128)(2,1)} fusion(bf16[2048,1536]{1,0:T(8,128)(2,1)} %get-tuple-element.63, bf16[1536,2048]{1,0:T(8,128)(2,1)S(1)} %copy-done.9), kind=kOutput, calls=%fused_computation.28 | convolution fusion | flops 9666035712 | bytes 17301504 | tf_op jit(solution)/shard_map/dot_general | solution.py:447
  653.4 222.3 %shard_map.477 = (f32[96,1536]{1,0:T(8,128)}, f32[96,768]{1,0:T(8,128)}, f32[96,2048]{1,0:T(8,128)}, f32[96,2048]{1,0:T(8,128)}, f32[96,2048]{1,0:T(8,128)}) custom-call(bf16[4,2,2,96,1536]{4,3,2,1,0:T(8,128)(2,1)} %bitcast.53, bf16[4,2,2,96,768]{4,3,2,1,0:T(8,128)(2,1)} %bitcast.54, bf16[4,2,2,96,2048]{4,3,2,1,0:T(8,128)(2,1)} %bitcast.52, ...), custom_call_target="tpu_custom_call" | custom-call | tf_op jit(solution)/shard_map/pallas_call | solution.py:351
  875.7 1.6 multiply_reduce_fusion.7
  877.3 1.8 multiply_reduce_fusion.6
  880.5 1.9 multiply_reduce_fusion.5
  883.1 1.9 multiply_reduce_fusion.4
  885.6 1.9 multiply_reduce_fusion.3
  888.3 9.0 fusion.7
  898.0 15.4 %shard_map.478 = f32[32,32,128]{2,1,0:T(8,128)} custom-call(f32[32,128]{1,0:T(8,128)} %concatenate.12.message_ref), custom_call_target="tpu_custom_call" | custom-call | tf_op jit(solution)/shard_map/pallas_call | solution.py:414
  913.4 1.5 slice_reduce_fusion.1
  914.9 1.0 slice_reduce_fusion
  918.0 3.6 multiply_subtract_fusion.2
  921.6 1.3 add_subtract_fusion.1
  922.9 2.5 multiply_subtract_fusion.4
  925.5 2.5 add_subtract_fusion
  928.1 3.1 multiply_subtract_fusion
  931.2 15.1 %fusion.6 = f32[2048,1536]{1,0:T(8,128)} fusion(f32[2048,1536]{1,0:T(8,128)} %get-tuple-element.101, bf16[2048,1536]{1,0:T(8,128)(2,1)S(1)} %bitcast.35, bf16[2048,1536]{1,0:T(8,128)(2,1)} %collective-permute-done.3, bf16[2048,1536]{1,0:T(8,128)(2,1)} %convolution_convert_fusion.1, f32[2048]{0:T(1024)S(1)} %broadcast_multiply_fusion, f32[1536]{0:T(1024)S(1)} %copy-done.21, ...), kind=kLoop, calls=%fused_computation.9 | loop fusion | flops 31457280 | bytes 44062720 | tf_op jit(solution)/shard_map/add | solution.py:798
  (101 shorter events, 5.1 us)
Async XLA Ops:
  323.1 10.5 %collective-permute-start = (bf16[2048,1536]{1,0:T(8,128)(2,1)}, bf16[2048,1536]{1,0:T(8,128)(2,1)}, u32[]{:S(2)}, u32[]{:S(2)}) collective-permute-start(bf16[2048,1536]{1,0:T(8,128)(2,1)} %convolution_convert_fusion), channel_id=1, source_target_pairs={{0,1},{1,0},{2,3},{3,2},{4,5},{5,4},{6,7},{7,6},{8,9},{9,8},{10,11... | collective-permute-start | bytes 18874376 | tf_op jit(solution)/shard_map/ppermute | solution.py:706
  447.6 59.1 %collective-permute-start.2 = (bf16[2048,1536]{1,0:T(8,128)(2,1)}, bf16[2048,1536]{1,0:T(8,128)(2,1)S(1)}, u32[]{:S(2)}, u32[]{:S(2)}) collective-permute-start(bf16[2048,1536]{1,0:T(8,128)(2,1)} %second_norm_grad.1), channel_id=1, source_target_pairs={{0,1},{1,0},{2,3},{3,2},{4,5},{5,4},{6,7},{7,6},{8,9},{9,8},{10,11... | collective-permute-start | bytes 18874376 | tf_op jit(solution)/shard_map/ppermute | solution.py:706
  467.0 45.0 %collective-permute-start.1 = (bf16[2048,1536]{1,0:T(8,128)(2,1)}, bf16[2048,1536]{1,0:T(8,128)(2,1)}, u32[]{:S(2)}, u32[]{:S(2)}) collective-permute-start(bf16[2048,1536]{1,0:T(8,128)(2,1)} %convolution_convert_fusion.2), channel_id=1, source_target_pairs={{0,1},{1,0},{2,3},{3,2},{4,5},{5,4},{6,7},{7,6},{8,9},{9,8},{10,11... | collective-permute-start | bytes 18874376 | tf_op jit(solution)/shard_map/ppermute | solution.py:706
  468.0 38.7 %slice-start = ((s8[12582912]{0:T(1024)(128)(4,1)}), s8[4194304]{0:T(1024)(128)(4,1)S(1)}, s32[]{:S(2)}) async-start(s8[12582912]{0:T(1024)(128)(4,1)} %bitcast.32), calls=%async_computation | async-start | bytes 8388608
  468.0 38.7 %slice-start.1 = ((s8[12582912]{0:T(1024)(128)(4,1)}), s8[4194304]{0:T(1024)(128)(4,1)S(1)}, s32[]{:S(2)}) async-start(s8[12582912]{0:T(1024)(128)(4,1)} %bitcast.32), calls=%async_computation.1 | async-start | bytes 8388608
  468.0 38.8 %slice-start.5 = ((s8[6291456]{0:T(1024)(128)(4,1)}), s8[4194304]{0:T(1024)(128)(4,1)S(1)}, s32[]{:S(2)}) async-start(s8[6291456]{0:T(1024)(128)(4,1)} %bitcast.36), calls=%async_computation.5 | async-start | bytes 8388608
  487.2 19.5 %slice-start.2 = ((s8[12582912]{0:T(1024)(128)(4,1)}), s8[4194304]{0:T(1024)(128)(4,1)S(1)}, s32[]{:S(2)}) async-start(s8[12582912]{0:T(1024)(128)(4,1)} %bitcast.32), calls=%async_computation.2 | async-start | bytes 8388608
  487.2 19.5 %slice-start.6 = ((s8[6291456]{0:T(1024)(128)(4,1)}), s8[2097152]{0:T(1024)(128)(4,1)S(1)}, s32[]{:S(2)}) async-start(s8[6291456]{0:T(1024)(128)(4,1)} %bitcast.36), calls=%async_computation.6 | async-start | bytes 4194304
  506.8 5.2 copy-start
  594.0 2.4 copy-start.11
  594.0 2.8 copy-start.10
  596.4 18.0 %slice-start.10 = ((s8[6291456]{0:T(1024)(128)(4,1)}), s8[4194304]{0:T(1024)(128)(4,1)S(1)}, s32[]{:S(2)}) async-start(s8[6291456]{0:T(1024)(128)(4,1)} %bitcast.40), calls=%async_computation.10 | async-start | bytes 8388608
  597.0 2.8 copy-start.8
  599.8 14.6 %slice-start.11 = ((s8[6291456]{0:T(1024)(128)(4,1)}), s8[2097152]{0:T(1024)(128)(4,1)S(1)}, s32[]{:S(2)}) async-start(s8[6291456]{0:T(1024)(128)(4,1)} %bitcast.40), calls=%async_computation.11 | async-start | bytes 4194304
  599.8 33.2 %slice-start.7 = ((s8[12582912]{0:T(1024)(128)(4,1)}), s8[4194304]{0:T(1024)(128)(4,1)S(1)}, s32[]{:S(2)}) async-start(s8[12582912]{0:T(1024)(128)(4,1)} %bitcast.38), calls=%async_computation.7 | async-start | bytes 8388608
  599.8 33.2 %slice-start.8 = ((s8[12582912]{0:T(1024)(128)(4,1)}), s8[4194304]{0:T(1024)(128)(4,1)S(1)}, s32[]{:S(2)}) async-start(s8[12582912]{0:T(1024)(128)(4,1)} %bitcast.38), calls=%async_computation.8 | async-start | bytes 8388608
  614.2 18.8 %slice-start.9 = ((s8[12582912]{0:T(1024)(128)(4,1)}), s8[4194304]{0:T(1024)(128)(4,1)S(1)}, s32[]{:S(2)}) async-start(s8[12582912]{0:T(1024)(128)(4,1)} %bitcast.38), calls=%async_computation.9 | async-start | bytes 8388608
  614.2 18.9 %copy-start.6 = (bf16[768,2048]{1,0:T(8,128)(2,1)S(1)}, bf16[768,2048]{1,0:T(8,128)(2,1)}, u32[]{:S(2)}) copy-start(bf16[768,2048]{1,0:T(8,128)(2,1)} %get-tuple-element.49.mixed_ref) | copy-start | bytes 9437188
  614.2 274.0 %collective-permute-start.3 = (bf16[2048,1536]{1,0:T(8,128)(2,1)}, bf16[2048,1536]{1,0:T(8,128)(2,1)}, u32[]{:S(2)}, u32[]{:S(2)}) collective-permute-start(bf16[2048,1536]{1,0:T(8,128)(2,1)} %convolution_convert_fusion.1), channel_id=1, source_target_pairs={{0,1},{1,0},{2,3},{3,2},{4,5},{5,4},{6,7},{7,6},{8,9},{9,8},{10,11... | collective-permute-start | bytes 18874376 | tf_op jit(solution)/shard_map/ppermute | solution.py:706
  633.1 6.6 copy-start.9
  653.4 234.8 %copy-start.21 = (f32[1536]{0:T(1024)S(1)}, f32[1536]{0:T(1024)}, u32[]{:S(2)}) copy-start(f32[1536]{0:T(1024)} %get-tuple-element.73) | copy-start | bytes 18436
  653.4 234.8 %copy-start.22 = (f32[2048]{0:T(1024)S(1)}, f32[2048]{0:T(1024)}, u32[]{:S(2)}) copy-start(f32[2048]{0:T(1024)} %add_rsqrt_fusion) | copy-start | bytes 24580
  888.3 29.7 %copy-start.1 = (f32[96,2048]{1,0:T(8,128)S(1)}, f32[96,2048]{1,0:T(8,128)}, u32[]{:S(2)}) copy-start(f32[96,2048]{1,0:T(8,128)} %param.36) | copy-start | bytes 2359300
  897.3 24.3 %copy-start.23 = (f32[2,96]{1,0:T(2,128)S(1)}, f32[2,96]{1,0:T(2,128)}, u32[]{:S(2)}) copy-start(f32[2,96]{1,0:T(2,128)} %param.55) | copy-start | bytes 2308
  897.3 24.3 %copy-start.24 = (f32[2,96]{1,0:T(2,128)S(1)}, f32[2,96]{1,0:T(2,128)}, u32[]{:S(2)}) copy-start(f32[2,96]{1,0:T(2,128)} %param.47) | copy-start | bytes 2308
  897.3 28.1 %copy-start.12 = (f32[96,768]{1,0:T(8,128)S(1)}, f32[96,768]{1,0:T(8,128)}, u32[]{:S(2)}) copy-start(f32[96,768]{1,0:T(8,128)} %param.35) | copy-start | bytes 884740
  897.3 30.7 %copy-start.2 = (f32[96,2048]{1,0:T(8,128)S(1)}, f32[96,2048]{1,0:T(8,128)}, u32[]{:S(2)}) copy-start(f32[96,2048]{1,0:T(8,128)} %param.37) | copy-start | bytes 2359300
  897.4 30.7 %copy-start.3 = (f32[96,2048]{1,0:T(8,128)S(1)}, f32[96,2048]{1,0:T(8,128)}, u32[]{:S(2)}) copy-start(f32[96,2048]{1,0:T(8,128)} %param.38) | copy-start | bytes 2359300
  897.4 30.6 %copy-start.4 = (f32[96,2048]{1,0:T(8,128)S(1)}, f32[96,2048]{1,0:T(8,128)}, u32[]{:S(2)}) copy-start(f32[96,2048]{1,0:T(8,128)} %get-tuple-element.67) | copy-start | bytes 2359300
  917.9 7.6 copy-start.7
  917.9 7.6 copy-start.13
  917.9 7.5 copy-start.14
  917.9 7.5 copy-start.19
  917.9 7.5 copy-start.20
  917.9 10.1 %copy-start.5 = (f32[96,2048]{1,0:T(8,128)S(1)}, f32[96,2048]{1,0:T(8,128)}, u32[]{:S(2)}) copy-start(f32[96,2048]{1,0:T(8,128)} %get-tuple-element.68) | copy-start | bytes 2359300
  917.9 10.1 %copy-start.15 = (f32[96,2048]{1,0:T(8,128)S(1)}, f32[96,2048]{1,0:T(8,128)}, u32[]{:S(2)}) copy-start(f32[96,2048]{1,0:T(8,128)} %param.54) | copy-start | bytes 2359300
  917.9 10.1 %copy-start.16 = (f32[96,2048]{1,0:T(8,128)S(1)}, f32[96,2048]{1,0:T(8,128)}, u32[]{:S(2)}) copy-start(f32[96,2048]{1,0:T(8,128)} %param.46) | copy-start | bytes 2359300
  918.0 10.1 %copy-start.17 = (f32[96,2048]{1,0:T(8,128)S(1)}, f32[96,2048]{1,0:T(8,128)}, u32[]{:S(2)}) copy-start(f32[96,2048]{1,0:T(8,128)} %param.53) | copy-start | bytes 2359300
  918.0 10.1 %copy-start.18 = (f32[96,2048]{1,0:T(8,128)S(1)}, f32[96,2048]{1,0:T(8,128)}, u32[]{:S(2)}) copy-start(f32[96,2048]{1,0:T(8,128)} %param.45) | copy-start | bytes 2359300
  922.9 8.3 slice-start.3
  928.1 3.1 slice-start.4

commit v2 on v1

v2 whole, which is shorter than its diff:
```python
import enum
import math

import jax
import jax.numpy as jnp
from jax import lax
from jax.experimental import pallas as pl
from jax.experimental.pallas import tpu as pltpu
from jax.sharding import PartitionSpec as P

HEAD_WIDTH = 96
GROUP_WIDTH = 2
SEQUENCE_LENGTH = 1024
QUERY_CHUNK = 512
VMEM_BYTES = 62 * 2**20
LOG2_E = 1.4426950408889634
SCORE_SCALE = 1.0 / math.sqrt(HEAD_WIDTH)

theta_base = 100000.0
norm_eps = 1e-05
beta_one = 0.9
beta_two = 0.95
adam_eps = 1e-08
decay_rate = 0.1
clip_limit = 1.0
neg_fill = -1e30
matrix_rates = (0.08, 0.08, 0.08, 1.0, 0.08, 0.08, 0.1)
gain_rate = 1.0

BF16 = jnp.bfloat16
F32 = jnp.float32
ANYWHERE = pl.BlockSpec(memory_space=pl.ANY)
MESH_ID = pl.DeviceIdType.MESH
GATHER_ORDERS = ((0, 1, 2), (2, 0, 1))
SCATTER_ORDERS = ((2, 1, 0), (1, 0, 2))
CHUNK = 256
PARTIAL_COLUMNS = 512


class Name(enum.Enum):
    block_in = enum.auto()
    block_out = enum.auto()
    change = enum.auto()
    cosine = enum.auto()
    dgate = enum.auto()
    dmiddle = enum.auto()
    dmixed = enum.auto()
    down_full = enum.auto()
    dqkv = enum.auto()
    dup = enum.auto()
    gain_sum = enum.auto()
    gains = enum.auto()
    gate = enum.auto()
    gate_full = enum.auto()
    grad_down = enum.auto()
    grad_gate = enum.auto()
    grad_out = enum.auto()
    grad_qkv = enum.auto()
    grad_up = enum.auto()
    hidden = enum.auto()
    logsums = enum.auto()
    middle = enum.auto()
    mixed = enum.auto()
    normed_one = enum.auto()
    normed_two = enum.auto()
    o_full = enum.auto()
    out_grad = enum.auto()
    prefix = enum.auto()
    qkv = enum.auto()
    qkv_full = enum.auto()
    share_gain = enum.auto()
    share_square = enum.auto()
    sine = enum.auto()
    square_sum = enum.auto()
    squares = enum.auto()
    sum_down = enum.auto()
    sum_gate = enum.auto()
    sum_out = enum.auto()
    sum_qkv = enum.auto()
    sum_up = enum.auto()
    swap = enum.auto()
    up = enum.auto()
    up_full = enum.auto()


def factor(count):
    return {16: (4, 2, 2), 64: (4, 4, 4)}.get(count, (count, 1, 1))


class Place:
    def __init__(self, dims):
        self.dims = dims
        mine = lax.axis_index("dp")
        n0, n1, n2 = dims
        self.at = (lax.rem(mine // (n1 * n2), n0), lax.rem(mine // n2, n1), lax.rem(mine, n2))

    def peer(self, dim, step):
        return lax.rem(self.at[dim] + step, self.dims[dim])

    def device(self, dim, coord):
        digits = list(self.at)
        digits[dim] = coord
        return {"dp": (digits[0] * self.dims[1] + digits[1]) * self.dims[2] + digits[2]}


def view(ref, fixed, columns):
    picks = tuple(fixed.get(d, slice(None)) for d in range(3))
    return ref.at[picks + (slice(None), pl.ds(columns[0], columns[1]))]


def entry_barrier(place):
    barrier = pltpu.get_barrier_semaphore()
    total = 0
    for dim in range(3):
        for step in range(1, place.dims[dim]):
            pl.semaphore_signal(
                barrier,
                inc=1,
                device_id=place.device(dim, place.peer(dim, step)),
                device_id_type=MESH_ID,
            )
            total += 1
    pl.semaphore_signal(
        barrier, inc=1, device_id={"tensor": 1 - lax.axis_index("tensor")}, device_id_type=MESH_ID
    )
    pl.semaphore_wait(barrier, total + 1)


class Exchange:
    def __init__(self, refs):
        self.own, self.other, self.send, self.recv, self.free = (
            refs[Name.swap, part] for part in range(5)
        )
        self.peer = {"tensor": 1 - lax.axis_index("tensor")}

    def copy(self, number, rows, columns):
        return pltpu.make_async_remote_copy(
            src_ref=self.own.at[rows, columns],
            dst_ref=self.other.at[rows, columns],
            send_sem=self.send.at[number],
            recv_sem=self.recv.at[number],
            device_id=self.peer,
            device_id_type=MESH_ID,
        )

    @staticmethod
    def release(refs):
        here = Exchange(refs)
        pl.semaphore_signal(here.free, inc=1, device_id=here.peer, device_id_type=MESH_ID)

    @staticmethod
    def claim(refs):
        pl.semaphore_wait(refs[Name.swap, 4], 1)

    @staticmethod
    def scratch(tokens, width, count):
        kinds = (
            pltpu.VMEM((tokens, width), BF16),
            pltpu.VMEM((tokens, width), BF16),
            pltpu.SemaphoreType.DMA((count,)),
            pltpu.SemaphoreType.DMA((count,)),
            pltpu.SemaphoreType.REGULAR,
        )
        return {(Name.swap, part): kind for part, kind in enumerate(kinds)}


class GatherChunk:
    def __init__(self, place, master, shard, full, columns, order, send, recv, local):
        self.place, self.shard, self.full, self.columns = place, shard, full, columns
        self.order, self.send, self.recv, self.local = order, send, recv, local
        self.master = master

    def copies(self, stage, arriving):
        place, dim, made = self.place, self.order[stage], []
        for step in range(1, place.dims[dim]):
            fixed = {d: place.at[d] for d in self.order[stage:]}
            if arriving:
                fixed[dim] = place.peer(dim, place.dims[dim] - step)
            target = view(self.full, fixed, self.columns)
            source = target
            if stage == 0 and not arriving:
                source = self.shard.at[:, pl.ds(*self.columns)]
            made.append(
                pltpu.make_async_remote_copy(
                    src_ref=source,
                    dst_ref=target,
                    send_sem=self.send.at[stage, step - 1],
                    recv_sem=self.recv.at[stage, step - 1],
                    device_id=place.device(dim, place.peer(dim, step)),
                    device_id_type=MESH_ID,
                )
            )
        return made

    def own(self):
        fixed = {d: self.place.at[d] for d in range(3)}
        return pltpu.make_async_copy(
            self.shard.at[:, pl.ds(*self.columns)],
            view(self.full, fixed, self.columns),
            self.local,
        )

    def act(self, phase):
        if phase == 0:
            columns = slice(self.columns[0], self.columns[0] + self.columns[1])
            self.shard[:, columns] = self.master[:, columns].astype(BF16)
            self.own().start()
        else:
            if phase == 1:
                self.own().wait()
            for copy in self.copies(phase - 1, True):
                copy.wait_recv()
        if phase < 3:
            for copy in self.copies(phase, False):
                copy.start()
        else:
            for stage in range(3):
                for copy in self.copies(stage, False):
                    copy.wait_send()


class ScatterChunk:
    def __init__(
        self, place, grad, out, squares, columns, order, mine, landings, send, recv, local
    ):
        self.place, self.grad, self.out, self.columns = place, grad, out, columns
        self.order, self.send, self.recv, self.local = order, send, recv, local
        self.squares, self.mine, self.landings = squares, mine, landings
        self.total = landings[0].at[0]
        self.rest = [d for d in range(3) if d != order[0]]

    def pick(self, second, third):
        return tuple(second if d == self.order[1] else third for d in self.rest)

    def copies(self, stage, arriving):
        place, dim, made = self.place, self.order[stage], []
        for step in range(1, place.dims[dim]):
            to = place.peer(dim, step)
            land = self.landings[stage].at[step - 1]
            if arriving:
                source = land
            elif stage == 0:
                source = view(self.grad, {dim: to}, self.columns)
            elif stage == 1:
                source = self.total.at[self.pick(to, slice(None))]
            else:
                source = self.total.at[self.pick(place.at[self.order[1]], to)]
            made.append(
                pltpu.make_async_remote_copy(
                    src_ref=source,
                    dst_ref=land,
                    send_sem=self.send.at[stage, step - 1],
                    recv_sem=self.recv.at[stage, step - 1],
                    device_id=place.device(dim, to),
                    device_id_type=MESH_ID,
                )
            )
        return made

    def own(self):
        first = self.order[0]
        return pltpu.make_async_copy(
            view(self.grad, {first: self.place.at[first]}, self.columns), self.mine, self.local
        )

    def act(self, phase):
        place, order = self.place, self.order
        if phase == 0:
            self.own().start()
        else:
            for copy in self.copies(phase - 1, True):
                copy.wait_recv()
        if phase == 1:
            self.own().wait()
            outer, inner = (place.dims[d] for d in self.rest)

            def add_first(item, carry):
                i, j = item // inner, lax.rem(item, inner)
                value = self.mine[i, j].astype(F32)
                for slot in range(place.dims[order[0]] - 1):
                    value = value + self.landings[0][slot, i, j].astype(F32)
                self.total[i, j] = value.astype(BF16)
                return carry

            lax.fori_loop(0, outer * inner, add_first, 0)
        if phase == 2:

            def add_second(item, carry):
                spot = self.pick(place.at[order[1]], item)
                value = self.total[spot].astype(F32)
                for slot in range(place.dims[order[1]] - 1):
                    value = value + self.landings[1][slot, item].astype(F32)
                self.total[spot] = value.astype(BF16)
                return carry

            lax.fori_loop(0, place.dims[order[2]], add_second, 0)
        if phase < 3:
            for copy in self.copies(phase, False):
                copy.start()
        else:
            value = self.total[self.pick(place.at[order[1]], place.at[order[2]])].astype(F32)
            for slot in range(place.dims[order[2]] - 1):
                value = value + self.landings[2][slot].astype(F32)
            self.out[:, self.columns[0] : self.columns[0] + self.columns[1]] = value
            self.squares[...] += jnp.sum(value * value, 0, keepdims=True)
            for stage in range(3):
                for copy in self.copies(stage, False):
                    copy.wait_send()


def chunks_of(widths):
    first, second = [], []
    for which, width in enumerate(widths):
        count = width // CHUNK
        later = max(1, round(count * 4 / 11))
        for i in range(count):
            (first if i < count - later else second).append((which, (i * CHUNK, CHUNK)))
    return first, second


def slots_of(first, second, stride=2):
    rows = []
    for slot in range(max(first, second) + 3 * stride):
        row = []
        for phase in (3, 2, 1, 0):
            if 0 <= slot - phase * stride < first:
                row.append((0, slot - phase * stride, phase))
            for chunk in range(second):
                if round(chunk * max(1, first) / max(1, second)) + phase * stride == slot:
                    row.append((1, chunk, phase))
        rows.append(row)
    return rows


class Gather:
    def __init__(self, shards, dims):
        self.dims, self.names = dims, list(shards)
        self.parts = [[part.shape[1] for part in parts] for parts in shards.values()]
        self.operands = [part for parts in shards.values() for part in parts]
        self.widths = [sum(widths) for widths in self.parts]
        self.rows = self.operands[0].shape[0]
        self.plan = chunks_of(self.widths)
        self.count = sum(len(p) for p in self.plan)
        self.slots = slots_of(*(len(p) for p in self.plan))
        self.in_specs = [ANYWHERE] * len(self.operands)
        self.out_specs = [ANYWHERE] * len(shards)
        self.out_shape = [
            jax.ShapeDtypeStruct(dims + (self.rows, width), BF16) for width in self.widths
        ]
        most = max(1, max(dims) - 1)
        self.scratch = [
            pltpu.SemaphoreType.DMA((self.count, 3, most)),
            pltpu.SemaphoreType.DMA((self.count, 3, most)),
            pltpu.SemaphoreType.DMA((self.count,)),
            pltpu.SemaphoreType.DMA((len(self.operands),)),
        ]
        self.scratch += [pltpu.VMEM((self.rows, width), F32) for width in self.widths]
        self.scratch += [pltpu.VMEM((self.rows, width), BF16) for width in self.widths]

    def begin(self, ins, outs, scratch):
        masters, number = scratch[4 : 4 + len(self.widths)], 0
        copies = []
        for master, widths in zip(masters, self.parts):
            first = 0
            for width in widths:
                copies.append(
                    pltpu.make_async_copy(
                        ins[number], master.at[:, pl.ds(first, width)], scratch[3].at[number]
                    )
                )
                first += width
                number += 1
        for copy in copies:
            copy.start()
        return lambda: [copy.wait() for copy in copies]

    def chunks(self, place, ins, outs, scratch):
        send, recv, local = scratch[:3]
        masters = scratch[4 : 4 + len(self.widths)]
        shards = scratch[4 + len(self.widths) :]
        made, number = [], 0
        for order, plan in zip(GATHER_ORDERS, self.plan):
            group = []
            for which, columns in plan:
                group.append(
                    GatherChunk(
                        place,
                        masters[which],
                        shards[which],
                        outs[which],
                        columns,
                        order,
                        send.at[number],
                        recv.at[number],
                        local.at[number],
                    )
                )
                number += 1
            made.append(group)
        return made


class Scatter:
    held = 3

    def __init__(self, grads, dims, rows):
        self.dims, self.rows = dims, rows
        self.sources = [source for source, _, _ in grads]
        self.widths = [width for _, width, _ in grads]
        self.names = [name for _, _, name in grads] + [Name.squares]
        self.operands, self.in_specs = [], []
        self.plan = chunks_of(self.widths)
        self.count = sum(len(p) for p in self.plan)
        self.slots = slots_of(*(len(p) for p in self.plan))
        self.out_specs = [pl.BlockSpec(memory_space=pltpu.VMEM)] * len(self.names)
        self.out_shape = [jax.ShapeDtypeStruct((rows, width), F32) for width in self.widths]
        self.out_shape.append(jax.ShapeDtypeStruct((1, CHUNK), F32))
        most = max(1, max(dims) - 1)
        self.scratch = [
            pltpu.SemaphoreType.DMA((self.count, 3, most)),
            pltpu.SemaphoreType.DMA((self.count, 3, most)),
            pltpu.SemaphoreType.DMA((self.count,)),
        ]
        for order, plan in zip(SCATTER_ORDERS, self.plan):
            c, b, a = order
            rest = tuple(dims[d] for d in range(3) if d != c)
            tile, count = (rows, CHUNK), max(1, len(plan))
            self.scratch.append(pltpu.VMEM((self.held,) + rest + tile, BF16))
            for lead in (
                (max(1, dims[c] - 1),) + rest,
                (max(1, dims[b] - 1), dims[a]),
                (max(1, dims[a] - 1),),
            ):
                self.scratch.append(pltpu.VMEM((count,) + lead + tile, BF16))

    def begin(self, ins, outs, scratch):
        outs[-1][...] = jnp.zeros_like(outs[-1])
        return lambda: None

    def chunks(self, place, grads, outs, scratch):
        send, recv, local = scratch[:3]
        made, number = [], 0
        for side, (order, plan) in enumerate(zip(SCATTER_ORDERS, self.plan)):
            buffers = scratch[3 + 4 * side : 7 + 4 * side]
            group = []
            for at, (which, columns) in enumerate(plan):
                group.append(
                    ScatterChunk(
                        place,
                        grads[which],
                        outs[which],
                        outs[-1],
                        columns,
                        order,
                        buffers[0].at[at % self.held],
                        [buffer.at[at] for buffer in buffers[1:]],
                        send.at[number],
                        recv.at[number],
                        local.at[number],
                    )
                )
                number += 1
            made.append(group)
        return made


def start_row(plan, which):
    for number, row in enumerate(plan.slots):
        for order, chunk, phase in row:
            if phase == 0 and plan.plan[order][chunk][0] in which:
                return number
    return len(plan.slots)


def done_row(plan, which):
    last = 0
    for number, row in enumerate(plan.slots):
        for order, chunk, phase in row:
            if phase == 3 and plan.plan[order][chunk][0] in which:
                last = number + 1
    return last


class Phase:
    def __init__(
        self,
        body,
        grid,
        in_specs,
        out_specs,
        inputs,
        outputs,
        before=0,
        until=0,
        enter=None,
        after=None,
    ):
        self.body, self.grid, self.enter, self.after = body, grid, enter, after
        self.in_specs, self.out_specs = in_specs, out_specs
        self.inputs, self.outputs = inputs, outputs
        self.before, self.until = before, until


class Everyone:
    def __init__(self, message, held, send, recv, across):
        self.message, self.held, self.send, self.recv = message, held, send, recv
        self.tensor = lax.axis_size("tensor")
        self.across = across
        dp = lax.axis_size("dp")
        self.total = dp * self.tensor if across else dp
        self.mine = lax.axis_index("dp")
        if across:
            self.mine = self.mine * self.tensor + lax.axis_index("tensor")

    def device(self, step):
        number = lax.rem(self.mine + step, self.total)
        if not self.across:
            return {"dp": number}
        return {"dp": number // self.tensor, "tensor": lax.rem(number, self.tensor)}

    def copy(self, step, slot):
        return pltpu.make_async_remote_copy(
            src_ref=self.message,
            dst_ref=self.held.at[slot],
            send_sem=self.send.at[step],
            recv_sem=self.recv.at[step],
            device_id=self.device(step),
            device_id_type=MESH_ID,
        )

    def start(self):
        def one(step, carry):
            self.copy(step, self.mine).start()
            return carry

        lax.fori_loop(1, self.total, one, 0)
        self.held[self.mine] = self.message[...]

    def finish(self):
        def one(step, carry):
            copy = self.copy(step, lax.rem(self.mine + self.total - step, self.total))
            copy.wait_recv()
            copy.wait_send()
            return carry

        lax.fori_loop(1, self.total, one, 0)

        def add(slot, carry):
            return carry + self.held[slot]

        return lax.fori_loop(0, self.total, add, jnp.zeros(self.message.shape, F32))

    @staticmethod
    def scratch(total, rows, columns):
        return [
            pltpu.VMEM((rows, columns), F32),
            pltpu.VMEM((total, rows, columns), F32),
            pltpu.SemaphoreType.DMA((total,)),
            pltpu.SemaphoreType.DMA((total,)),
        ]


def greet_all():
    tensor = lax.axis_size("tensor")
    total = lax.axis_size("dp") * tensor
    mine = lax.axis_index("dp") * tensor + lax.axis_index("tensor")
    barrier = pltpu.get_barrier_semaphore()

    def greet(step, carry):
        number = lax.rem(mine + step, total)
        pl.semaphore_signal(
            barrier,
            inc=1,
            device_id={"dp": number // tensor, "tensor": lax.rem(number, tensor)},
            device_id_type=MESH_ID,
        )
        return carry

    lax.fori_loop(1, total, greet, 0)
    pl.semaphore_wait(barrier, total - 1)


def chain(
    name, phases, arrays, small, results, small_results, scratch, plan, collective_id, finish=None
):
    groups = [
        (False, list(arrays)),
        (False, list(small)),
        (True, len(plan.in_specs)),
        (False, list(results)),
        (False, list(small_results)),
        (True, len(plan.out_specs)),
        (False, list(scratch)),
        (True, len(plan.scratch)),
    ]

    def kernel(*everything):
        refs, lists, at = {}, [], 0
        for planned, group in groups:
            if planned:
                lists.append(list(everything[at : at + group]))
                at += group
                continue
            for label in group:
                refs[label] = everything[at]
                at += 1
        refs |= dict(zip(plan.names, lists[1]))
        place = Place(plan.dims)
        ready = plan.begin(*lists)
        if finish is None:
            entry_barrier(place)
        else:
            greet_all()
        ready()
        ins = lists[0]
        if isinstance(plan, Scatter):
            ins = [refs[source] for source in plan.sources]
        chunks = plan.chunks(place, ins, *lists[1:])

        def run(first, last):
            for row in plan.slots[first:last]:
                for order, chunk, phase in row:
                    chunks[order][chunk].act(phase)

        def find(label):
            return refs[label[0]].at[label[1]] if isinstance(label, tuple) else refs[label]

        done = 0
        for phase in phases:
            run(done, phase.before)
            done = max(done, phase.before)
            until = max(done, phase.until)
            if phase.enter is not None:
                phase.enter(refs)
            steps = math.prod(phase.grid)
            marks = [done + (until - done) * number // steps for number in range(steps + 1)]

            def body(*blocks, phase=phase, marks=marks, steps=steps):
                index = tuple(pl.program_id(axis) for axis in range(len(phase.grid)))
                step = 0
                for position, extent in zip(index, phase.grid):
                    step = step * extent + position
                for number in range(steps):
                    if marks[number] < marks[number + 1]:

                        @pl.when(step == number)
                        def _(number=number):
                            run(marks[number], marks[number + 1])

                phase.body(refs, index, *blocks)

            pltpu.emit_pipeline(
                body, grid=phase.grid, in_specs=phase.in_specs, out_specs=phase.out_specs
            )(*(find(label) for label in (*phase.inputs, *phase.outputs)))
            done = until
            if phase.after is not None:
                phase.after(refs)
        run(done, len(plan.slots))
        if finish is not None:
            finish(refs)

    in_vmem = pl.BlockSpec(memory_space=pltpu.VMEM)
    outs = pl.pallas_call(
        kernel,
        name=name,
        in_specs=[ANYWHERE] * len(arrays) + [spec for _, spec in small.values()] + plan.in_specs,
        out_specs=[ANYWHERE] * len(results) + [in_vmem] * len(small_results) + plan.out_specs,
        out_shape=[*results.values(), *small_results.values(), *plan.out_shape],
        scratch_shapes=[*scratch.values(), *plan.scratch],
        compiler_params=pltpu.CompilerParams(
            collective_id=collective_id, has_side_effects=True, vmem_limit_bytes=VMEM_BYTES
        ),
    )(*arrays.values(), *(array for array, _ in small.values()), *plan.operands)
    return dict(zip([*results, *small_results, *plan.names], outs))


def rotary_tables():
    half_size = HEAD_WIDTH // 2
    frequency = jnp.power(
        theta_base, -2.0 * jnp.arange(half_size, dtype=F32) / HEAD_WIDTH
    )
    angles = frequency[:, None] * jnp.arange(SEQUENCE_LENGTH, dtype=F32)[None, :]
    return jnp.cos(angles), jnp.sin(angles)


def rotate(values, cosine, sine, sign):
    half = HEAD_WIDTH // 2
    top, bottom = values[:half], values[half:]
    return jnp.concatenate(
        [top * cosine - sign * (bottom * sine), bottom * cosine + sign * (top * sine)], 0
    )


def product(left, right, left_dim=1, right_dim=0):
    return lax.dot_general(
        left, right, (((left_dim,), (right_dim,)), ((), ())), preferred_element_type=F32
    )


def row_scale(values):
    return lax.rsqrt(jnp.mean(values * values, -1, keepdims=True) + norm_eps)


def whole(shape):
    return pl.BlockSpec(tuple(shape), lambda *index: (0,) * len(shape))


def out_like(*shape, dtype=BF16):
    return jax.ShapeDtypeStruct(shape, dtype)


def visible(prefix, first):
    place = lax.broadcasted_iota(jnp.int32, (1, QUERY_CHUNK), 1) + first
    limit = jnp.maximum(place + 1, prefix)
    return lax.broadcasted_iota(jnp.int32, (SEQUENCE_LENGTH, QUERY_CHUNK), 0) < limit


def project_phase(tokens, width, features, full_shape, **timing):
    block = 512
    turned = features * 3 // 4
    per_sequence = SEQUENCE_LENGTH // block

    def body(refs, index, x_ref, w_ref, cos_ref, sin_ref, n_ref, out_ref):
        x = x_ref[...].astype(F32)
        normed = (x * row_scale(x) * refs[Name.gains][:1]).astype(BF16)
        n_ref[...] = normed
        raw = product(w_ref[...].reshape(width, features), normed, 0, 1)
        cosine, sine = cos_ref[...], sin_ref[...]
        for first in range(0, turned, HEAD_WIDTH):
            rows = slice(first, first + HEAD_WIDTH)
            out_ref[rows] = rotate(raw[rows], cosine, sine, 1.0).astype(BF16)
        out_ref[turned:] = raw[turned:].astype(BF16)

    table = pl.BlockSpec((HEAD_WIDTH // 2, block), lambda i: (0, lax.rem(i, per_sequence)))
    rows = pl.BlockSpec((block, width), lambda i: (i, 0))
    return Phase(
        body,
        (tokens // block,),
        [rows, whole(full_shape), table, table],
        [rows, pl.BlockSpec((features, block), lambda i: (0, i))],
        [Name.block_in, Name.qkv_full, Name.cosine, Name.sine],
        [Name.normed_one, Name.qkv],
        **timing,
    )


def attention_specs(features):
    kv_heads = features // HEAD_WIDTH // (GROUP_WIDTH + 2)
    q_heads = kv_heads * GROUP_WIDTH
    wide = (GROUP_WIDTH * HEAD_WIDTH, SEQUENCE_LENGTH)
    slim = (HEAD_WIDTH, SEQUENCE_LENGTH)
    query = pl.BlockSpec(wide, lambda s, j: (j, s))
    key = pl.BlockSpec(slim, lambda s, j: (q_heads + j, s))
    value = pl.BlockSpec(slim, lambda s, j: (q_heads + kv_heads + j, s))
    sums = pl.BlockSpec((None, GROUP_WIDTH, SEQUENCE_LENGTH), lambda s, j: (j, 0, s))
    return kv_heads, query, key, value, sums


def attend_forward_phase(tokens, features, **timing):
    kv_heads, query, key, value, sums = attention_specs(features)
    scale = SCORE_SCALE * LOG2_E

    def body(refs, index, q_ref, k_ref, v_ref, mixed_ref, sum_ref):
        prefix = refs[Name.prefix][index[0]]
        keys = k_ref[...].T
        values = jnp.concatenate([v_ref[...], jnp.ones((16, SEQUENCE_LENGTH), BF16)], 0)
        for head in range(GROUP_WIDTH):
            rows = slice(head * HEAD_WIDTH, (head + 1) * HEAD_WIDTH)
            for first in range(0, SEQUENCE_LENGTH, QUERY_CHUNK):
                columns = slice(first, first + QUERY_CHUNK)
                scores = product(keys, q_ref[rows, columns])
                scores = jnp.where(visible(prefix, first), scores, neg_fill)
                peak = jnp.max(scores, 0, keepdims=True) * scale
                weights = jnp.exp2(scores * scale - peak).astype(BF16)
                out = product(values, weights)
                total = out[HEAD_WIDTH : HEAD_WIDTH + 1]
                mixed_ref[rows, columns] = (out[:HEAD_WIDTH] * (1.0 / total)).astype(BF16)
                sum_ref[head : head + 1, columns] = peak + jnp.log2(total)

    return Phase(
        body,
        (tokens // SEQUENCE_LENGTH, kv_heads),
        [query, key, value],
        [query, sums],
        [Name.qkv, Name.qkv, Name.qkv],
        [Name.mixed, Name.logsums],
        **timing,
    )


def attend_backward_phase(tokens, features, **timing):
    kv_heads, query, key, value, sums = attention_specs(features)
    scale = SCORE_SCALE * LOG2_E

    def body(
        refs,
        index,
        q_ref,
        k_ref,
        v_ref,
        d_ref,
        mixed_ref,
        sum_ref,
        cos_ref,
        sin_ref,
        dq_ref,
        dk_ref,
        dv_ref,
    ):
        prefix = refs[Name.prefix][index[0]]
        keys_flat = k_ref[...]
        keys, values = keys_flat.T, v_ref[...].T
        dkeys = jnp.zeros((SEQUENCE_LENGTH, HEAD_WIDTH), F32)
        dvalues = jnp.zeros((SEQUENCE_LENGTH, HEAD_WIDTH), F32)
        cosine, sine = cos_ref[...], sin_ref[...]
        for head in range(GROUP_WIDTH):
            rows = slice(head * HEAD_WIDTH, (head + 1) * HEAD_WIDTH)
            for first in range(0, SEQUENCE_LENGTH, QUERY_CHUNK):
                columns = slice(first, first + QUERY_CHUNK)
                q, d = q_ref[rows, columns], d_ref[rows, columns]
                delta = jnp.sum(
                    d.astype(F32) * mixed_ref[rows, columns].astype(F32), 0, keepdims=True
                )
                scores = product(keys, q) * scale
                weights = jnp.exp2(scores - sum_ref[head : head + 1, columns])
                weights = jnp.where(visible(prefix, first), weights, 0.0)
                dweights = product(values, d)
                dscores = (weights * (dweights - delta)).astype(BF16)
                dvalues = dvalues + product(weights.astype(BF16), d.T)
                dkeys = dkeys + product(dscores, q.T)
                dq = product(keys_flat, dscores) * SCORE_SCALE
                dq_ref[rows, columns] = rotate(
                    dq, cosine[:, columns], sine[:, columns], -1.0
                ).astype(BF16)
        dk_ref[...] = rotate((dkeys * SCORE_SCALE).T, cosine, sine, -1.0).astype(BF16)
        dv_ref[...] = dvalues.T.astype(BF16)

    slim = pl.BlockSpec((HEAD_WIDTH, SEQUENCE_LENGTH), lambda s, j: (j, s))
    table = whole((HEAD_WIDTH // 2, SEQUENCE_LENGTH))
    q_features, kv_features = features // 2, features // 4
    return Phase(
        body,
        (tokens // SEQUENCE_LENGTH, kv_heads),
        [query, key, value, query, query, sums, table, table],
        [query, slim, slim],
        [Name.qkv, Name.qkv, Name.qkv, Name.dmixed, Name.mixed, Name.logsums, Name.cosine, Name.sine],
        [
            (Name.dqkv, pl.ds(0, q_features)),
            (Name.dqkv, pl.ds(q_features, kv_features)),
            (Name.dqkv, pl.ds(q_features + kv_features, kv_features)),
        ],
        **timing,
    )


def attention_out_phase(tokens, width, full_shape, **timing):
    block = 256
    features = full_shape[-1]

    def body(refs, index, mixed_ref, w_ref):
        exchange = Exchange(refs)
        rows = pl.ds(pl.multiple_of(index[0] * block, block), block)
        value = product(mixed_ref[...], w_ref[...].reshape(width, features), 0, 1)
        exchange.own[rows, :] = value.astype(BF16)
        exchange.copy(index[0], rows, pl.ds(0, width)).start()

    return Phase(
        body,
        (tokens // block,),
        [pl.BlockSpec((features, block), lambda i: (0, i)), whole(full_shape)],
        [],
        [Name.mixed, Name.o_full],
        [],
        **timing,
    )


def received(refs, index, tokens, width, wide):
    block = 256
    exchange = Exchange(refs)
    rows = pl.ds(pl.multiple_of(index * block, block), block)
    for part in range(width // wide):
        copy = exchange.copy(part * (tokens // block) + index, rows, pl.ds(part * wide, wide))
        copy.wait_recv()
        copy.wait_send()
    return exchange.own[rows, :].astype(F32) + exchange.other[rows, :].astype(F32)


def row_blocks(width):
    return pl.BlockSpec((256, width), lambda i: (i, 0))


def second_norm_phase(tokens, width, **timing):
    def body(refs, index, x_ref, middle_ref, n_ref):
        attn = received(refs, index[0], tokens, width, width)
        middle = x_ref[...].astype(F32) + attn
        middle_ref[...] = middle.astype(BF16)
        n_ref[...] = (middle * row_scale(middle) * refs[Name.gains][1:]).astype(BF16)

    rows = row_blocks(width)
    return Phase(
        body,
        (tokens // 256,),
        [rows],
        [rows, rows],
        [Name.block_in],
        [Name.middle, Name.normed_two],
        **timing,
    )


def feed_forward_phase(tokens, lead, units, **timing):
    tall, wide = 1024, 512
    width = math.prod(lead)

    def body(refs, index, n_ref, gate_w, up_w, gate_ref, up_ref, hidden_ref):
        normed = n_ref[...]
        gate = product(normed, gate_w[...].reshape(width, wide))
        up = product(normed, up_w[...].reshape(width, wide))
        gate_ref[...] = gate.astype(BF16)
        up_ref[...] = up.astype(BF16)
        hidden_ref[...] = (gate * jax.nn.sigmoid(gate) * up).astype(BF16)

    weight = pl.BlockSpec(lead + (wide,), lambda i, j: (0, 0, 0, 0, j))
    out = pl.BlockSpec((tall, wide), lambda i, j: (i, j))
    return Phase(
        body,
        (tokens // tall, units // wide),
        [pl.BlockSpec((tall, width), lambda i, j: (i, 0)), weight, weight],
        [out, out, out],
        [Name.normed_two, Name.gate_full, Name.up_full],
        [Name.gate, Name.up, Name.hidden],
        **timing,
    )


def feed_backward_phase(tokens, width, units, **timing):
    tall, wide = 512, 512

    def body(refs, index, d_ref, down_w, gate_ref, up_ref, dgate_ref, dup_ref):
        dhidden = product(d_ref[...], down_w[...])
        gate = gate_ref[...].astype(F32)
        sigmoid = jax.nn.sigmoid(gate)
        dup_ref[...] = (dhidden * gate * sigmoid).astype(BF16)
        dgate_ref[...] = (
            dhidden * up_ref[...].astype(F32) * sigmoid * (1.0 + gate * (1.0 - sigmoid))
        ).astype(BF16)

    tile = pl.BlockSpec((tall, wide), lambda i, j: (i, j))
    return Phase(
        body,
        (tokens // tall, units // wide),
        [
            pl.BlockSpec((tall, width), lambda i, j: (i, 0)),
            pl.BlockSpec((width, wide), lambda i, j: (0, j)),
            tile,
            tile,
        ],
        [tile, tile],
        [Name.out_grad, Name.down_full, Name.gate, Name.up],
        [Name.dgate, Name.dup],
        **timing,
    )


def weight_grad_phase(tokens, lead, columns, inputs, output, wide, flat=False, **timing):
    tiles = 2
    tall = math.prod(lead) // tiles

    def body(refs, index, left_ref, right_ref, out_ref):
        value = product(left_ref[...], right_ref[...], 0, 1 if flat else 0)
        out_ref[...] = value.astype(BF16).reshape(out_ref.shape)

    right = (
        pl.BlockSpec((wide, tokens), lambda i, j: (j, 0))
        if flat
        else pl.BlockSpec((tokens, wide), lambda i, j: (0, j))
    )
    out = pl.BlockSpec((lead[0] // tiles,) + lead[1:] + (wide,), lambda i, j: (i, 0, 0, 0, j))
    return Phase(
        body,
        (tiles, columns // wide),
        [pl.BlockSpec((tokens, tall), lambda i, j: (0, i)), right],
        [out],
        inputs,
        [output],
        **timing,
    )


def partial_rows_phase(tokens, width, terms, **timing):
    block, wide = 256, PARTIAL_COLUMNS

    def body(refs, index, *blocks):
        exchange = Exchange(refs)
        value = 0.0
        for number, (_, _, depth, flat) in enumerate(terms):
            left, right = blocks[2 * number : 2 * number + 2]
            value = value + product(left[...], right[...], 0 if flat else 1, 1)
        rows = pl.ds(pl.multiple_of(index[1] * block, block), block)
        columns = pl.ds(pl.multiple_of(index[0] * wide, wide), wide)
        exchange.own[rows, columns] = value.astype(BF16)
        exchange.copy(index[0] * (tokens // block) + index[1], rows, columns).start()

    specs, inputs = [], []
    for left, right, depth, flat in terms:
        specs.append(
            pl.BlockSpec((depth, block), lambda n, i: (0, i))
            if flat
            else pl.BlockSpec((block, depth), lambda n, i: (i, 0))
        )
        specs.append(pl.BlockSpec((wide, depth), lambda n, i: (n, 0)))
        inputs += [left, right]
    return Phase(body, (width // wide, tokens // block), specs, [], inputs, [], **timing)


def add_gain(refs, row, index, value):
    total = refs[Name.share_gain, 0]

    @pl.when(index == 0)
    def _():
        total[row : row + 1] = jnp.zeros_like(total[row : row + 1])

    total[row : row + 1] += jnp.sum(value, 0, keepdims=True)


def norm_back_phase(tokens, width, row, inputs, output, add, **timing):
    def body(refs, index, row_ref, back_ref, out_ref):
        dnorm = received(refs, index[0], tokens, width, PARTIAL_COLUMNS)
        values = row_ref[...].astype(F32)
        inverse = row_scale(values)
        unit = values * inverse
        add_gain(refs, row, index[0], dnorm * unit)
        change = norm_back(dnorm, refs[Name.gains][row : row + 1], unit, inverse)
        if add:
            change = change + back_ref[...].astype(F32)
        out_ref[...] = change.astype(BF16)

    rows = row_blocks(width)
    return Phase(body, (tokens // 256,), [rows, rows], [rows], inputs, [output], **timing)


def block_out_phase(tokens, width, **timing):
    def body(refs, index, middle_ref, out_ref):
        ffn = received(refs, index[0], tokens, width, PARTIAL_COLUMNS)
        out_ref[...] = (middle_ref[...].astype(F32) + ffn).astype(BF16)

    rows = row_blocks(width)
    return Phase(
        body, (tokens // 256,), [rows], [rows], [Name.middle], [Name.block_out], **timing
    )


def mixed_grad_phase(tokens, width, features, **timing):
    block = 512

    def body(refs, index, w_ref, d_ref, out_ref):
        out_ref[...] = product(w_ref[...], d_ref[...], 0, 1).astype(BF16)

    return Phase(
        body,
        (tokens // block,),
        [whole((width, features)), pl.BlockSpec((block, width), lambda i: (i, 0))],
        [pl.BlockSpec((features, block), lambda i: (0, i))],
        [Name.o_full, Name.dmiddle],
        [Name.dmixed],
        **timing,
    )


def norm_back(dnorm, gain_row, unit_rows, inverse):
    scaled = dnorm * gain_row
    return inverse * (scaled - unit_rows * jnp.mean(scaled * unit_rows, -1, keepdims=True))


def adam_step(weight, gradient, first_moment, second_moment, rate, decay, factor, fix_one, fix_two):
    clipped = factor * gradient
    first_new = beta_one * first_moment + (1.0 - beta_one) * clipped
    second_new = beta_two * second_moment + (1.0 - beta_two) * clipped * clipped
    update = first_new / fix_one / (jnp.sqrt(second_new / fix_two) + adam_eps) + decay * weight
    return (weight - rate * update, first_new, second_new)


def local(
    block_in,
    prefix_len,
    out_grad,
    step_count,
    q_weight,
    key_matrix,
    value_matrix,
    o_weight,
    gate_weight,
    up_weight,
    down_weight,
    norm_gains,
    query_mean_moment,
    key_mean_moment,
    value_mean_moment,
    output_mean_moment,
    gate_mean_moment,
    up_mean_moment,
    down_mean_moment,
    gains_mean_moment,
    q_second,
    key_square_moment,
    value_square_moment,
    o_second,
    gate_second,
    up_second,
    down_second,
    gains_second,
):
    dims = factor(lax.axis_size("dp"))
    width = block_in.shape[1]
    q_width, kv_width = q_weight.shape[1], key_matrix.shape[1]
    units = gate_weight.shape[1]
    tokens = block_in.shape[0]
    features = q_width + 2 * kv_width
    blocks = tokens // 256
    rows = q_weight.shape[0]
    lead = dims + (rows,)
    devices = lax.axis_size("dp")
    cosine, sine = rotary_tables()
    gains = (norm_gains, pl.BlockSpec(memory_space=pltpu.VMEM))
    prefix = (prefix_len, pl.BlockSpec(memory_space=pltpu.SMEM))
    per_token = out_like(tokens, width)
    per_unit = out_like(tokens, units)

    plan = Gather(
        {
            Name.qkv_full: [q_weight, key_matrix, value_matrix],
            Name.o_full: [o_weight],
            Name.gate_full: [gate_weight],
            Name.up_full: [up_weight],
            Name.down_full: [down_weight],
        },
        dims,
    )
    first = done_row(plan, (0,))
    then = done_row(plan, (1,))
    later = done_row(plan, (2, 3))
    made = chain(
        "forward",
        [
            project_phase(
                tokens, width, features, lead + (features,), before=first, until=first + 2
            ),
            attend_forward_phase(tokens, features, until=max(then, first + 8)),
            attention_out_phase(
                tokens, width, lead + (q_width,), before=then, until=(first + 8 + later) // 2
            ),
            second_norm_phase(tokens, width, until=later),
            feed_forward_phase(tokens, lead, units, before=later, until=len(plan.slots) - 2),
            weight_grad_phase(
                tokens,
                lead,
                units,
                [Name.out_grad, Name.hidden],
                Name.grad_down,
                1024,
                until=len(plan.slots),
            ),
        ],
        {
            Name.block_in: block_in,
            Name.cosine: cosine,
            Name.sine: sine,
            Name.out_grad: out_grad,
        },
        {Name.gains: gains, Name.prefix: prefix},
        {
            Name.normed_one: per_token,
            Name.qkv: out_like(features, tokens),
            Name.mixed: out_like(q_width, tokens),
            Name.logsums: out_like(kv_width // HEAD_WIDTH, GROUP_WIDTH, tokens, dtype=F32),
            Name.middle: per_token,
            Name.normed_two: per_token,
            Name.gate: per_unit,
            Name.up: per_unit,
            Name.hidden: per_unit,
            Name.grad_down: out_like(*lead, units),
        },
        {},
        Exchange.scratch(tokens, width, blocks),
        plan,
        0,
    )
    for name in (Name.qkv_full, Name.o_full, Name.gate_full, Name.up_full, Name.down_full):
        made[name] = made[name].reshape(width, -1)

    plan = Scatter(
        [
            (Name.grad_down, units, Name.sum_down),
            (Name.grad_gate, units, Name.sum_gate),
            (Name.grad_up, units, Name.sum_up),
            (Name.grad_out, q_width, Name.sum_out),
            (Name.grad_qkv, features, Name.sum_qkv),
        ],
        dims,
        rows,
    )
    gate_row, up_row, out_row, qkv_row = (start_row(plan, (which,)) for which in range(1, 5))
    last = len(plan.slots)

    def share_gains(refs):
        Everyone(*(refs[Name.share_gain, part] for part in range(4)), False).start()
        Exchange.release(refs)

    def share_squares(refs):
        refs[Name.gain_sum][...] = Everyone(
            *(refs[Name.share_gain, part] for part in range(4)), False
        ).finish()
        everyone = Everyone(*(refs[Name.share_square, part] for part in range(4)), True)
        everyone.message[...] = refs[Name.squares][...]
        everyone.start()
        refs[Name.square_sum][...] = everyone.finish()

    scratch = Exchange.scratch(tokens, width, blocks * (width // PARTIAL_COLUMNS))
    for part, kind in enumerate(Everyone.scratch(devices, 2, width)):
        scratch[Name.share_gain, part] = kind
    for part, kind in enumerate(
        Everyone.scratch(devices * lax.axis_size("tensor"), 1, CHUNK)
    ):
        scratch[Name.share_square, part] = kind
    kept = (
        Name.down_full,
        Name.gate,
        Name.up,
        Name.normed_two,
        Name.gate_full,
        Name.up_full,
        Name.middle,
        Name.o_full,
        Name.qkv,
        Name.mixed,
        Name.logsums,
        Name.normed_one,
        Name.qkv_full,
        Name.hidden,
        Name.grad_down,
    )
    made |= chain(
        "backward",
        [
            feed_backward_phase(tokens, width, units, until=gate_row // 2),
            weight_grad_phase(
                tokens,
                lead,
                units,
                [Name.normed_two, Name.dgate],
                Name.grad_gate,
                512,
                until=gate_row,
            ),
            weight_grad_phase(
                tokens,
                lead,
                units,
                [Name.normed_two, Name.dup],
                Name.grad_up,
                512,
                until=min(up_row, gate_row + 2),
            ),
            partial_rows_phase(
                tokens,
                width,
                [
                    (Name.dgate, Name.gate_full, units, False),
                    (Name.dup, Name.up_full, units, False),
                ],
                until=gate_row + 6,
            ),
            norm_back_phase(
                tokens,
                width,
                1,
                [Name.middle, Name.out_grad],
                Name.dmiddle,
                True,
                until=gate_row + 7,
                after=Exchange.release,
            ),
            mixed_grad_phase(tokens, width, q_width, until=gate_row + 8),
            weight_grad_phase(
                tokens,
                lead,
                q_width,
                [Name.dmiddle, Name.mixed],
                Name.grad_out,
                q_width,
                flat=True,
                until=out_row,
            ),
            attend_backward_phase(tokens, features, until=qkv_row),
            weight_grad_phase(
                tokens, lead, features, [Name.normed_one, Name.dqkv], Name.grad_qkv, 768, flat=True
            ),
            partial_rows_phase(
                tokens,
                width,
                [(Name.dqkv, Name.qkv_full, features, True)],
                until=qkv_row + 3,
                enter=Exchange.claim,
            ),
            norm_back_phase(
                tokens,
                width,
                0,
                [Name.block_in, Name.dmiddle],
                Name.change,
                False,
                until=qkv_row + 4,
                after=share_gains,
            ),
            partial_rows_phase(
                tokens,
                width,
                [(Name.hidden, Name.down_full, units, False)],
                until=qkv_row + 7,
                enter=Exchange.claim,
            ),
            block_out_phase(tokens, width, until=qkv_row + 8),
        ],
        {
            Name.out_grad: out_grad,
            Name.block_in: block_in,
            Name.cosine: cosine,
            Name.sine: sine,
        }
        | {name: made[name] for name in kept},
        {Name.gains: gains, Name.prefix: prefix},
        {
            Name.dgate: per_unit,
            Name.dup: per_unit,
            Name.grad_gate: out_like(*lead, units),
            Name.grad_up: out_like(*lead, units),
            Name.dmiddle: per_token,
            Name.dmixed: out_like(q_width, tokens),
            Name.grad_out: out_like(*lead, q_width),
            Name.dqkv: out_like(features, tokens),
            Name.grad_qkv: out_like(*lead, features),
            Name.change: per_token,
            Name.block_out: per_token,
        },
        {
            Name.gain_sum: out_like(2, width, dtype=F32),
            Name.square_sum: out_like(1, CHUNK, dtype=F32),
        },
        scratch,
        plan,
        1,
        share_squares,
    )
    sum_qkv, sum_out, sum_gate, sum_up, sum_down = (
        made[name]
        for name in (Name.sum_qkv, Name.sum_out, Name.sum_gate, Name.sum_up, Name.sum_down)
    )
    block_out = made[Name.block_out]
    in_grad = made[Name.dmiddle].astype(F32) + made[Name.change].astype(F32)
    gain_sum = made[Name.gain_sum]
    total_square = jnp.sum(made[Name.square_sum]) + jnp.sum(jnp.square(gain_sum))
    gain_width = width // devices
    first_column = lax.axis_index("dp") * gain_width
    grad_gains = lax.dynamic_slice_in_dim(gain_sum, first_column, gain_width, 1)
    old_gains = lax.dynamic_slice_in_dim(norm_gains, first_column, gain_width, 1)
    reduced = (
        sum_qkv[:, :q_width],
        sum_qkv[:, q_width : q_width + kv_width],
        sum_qkv[:, q_width + kv_width :],
        sum_out,
        sum_gate,
        sum_up,
        sum_down,
        grad_gains,
    )
    grad_norm = jnp.sqrt(total_square)
    factor_now = jnp.minimum(1.0, clip_limit / grad_norm)
    step_float = step_count[0].astype(F32)
    fix_one = 1.0 - jnp.power(beta_one, step_float)
    fix_two = 1.0 - jnp.power(beta_two, step_float)
    masters = (
        q_weight,
        key_matrix,
        value_matrix,
        o_weight,
        gate_weight,
        up_weight,
        down_weight,
        old_gains,
    )
    firsts = (
        query_mean_moment,
        key_mean_moment,
        value_mean_moment,
        output_mean_moment,
        gate_mean_moment,
        up_mean_moment,
        down_mean_moment,
        gains_mean_moment,
    )
    seconds = (
        q_second,
        key_square_moment,
        value_square_moment,
        o_second,
        gate_second,
        up_second,
        down_second,
        gains_second,
    )
    rate_list = matrix_rates + (gain_rate,)
    decay_list = (decay_rate,) * 7 + (0.0,)
    new_weights, new_firsts, new_seconds = ([], [], [])
    for weight, gradient, first_moment, second_moment, rate, decay in zip(
        masters, reduced, firsts, seconds, rate_list, decay_list
    ):
        weight_new, first_new, second_new = adam_step(
            weight, gradient, first_moment, second_moment, rate, decay, factor_now, fix_one, fix_two
        )
        new_weights.append(weight_new)
        new_firsts.append(first_new)
        new_seconds.append(second_new)
    return (
        block_out,
        in_grad,
        grad_norm.reshape(1),
        new_weights[0],
        new_weights[1],
        new_weights[2],
        new_weights[3],
        new_weights[4],
        new_weights[5],
        new_weights[6],
        new_weights[7],
        new_firsts[0],
        new_firsts[1],
        new_firsts[2],
        new_firsts[3],
        new_firsts[4],
        new_firsts[5],
        new_firsts[6],
        new_firsts[7],
        new_seconds[0],
        new_seconds[1],
        new_seconds[2],
        new_seconds[3],
        new_seconds[4],
        new_seconds[5],
        new_seconds[6],
        new_seconds[7],
    )


def solution(mesh):
    return jax.shard_map(
        local,
        mesh=mesh,
        in_specs=(
            P("dp", None),
            P("dp"),
            P("dp", None),
            P(),
            P("dp", "tensor"),
            P("dp", "tensor"),
            P("dp", "tensor"),
            P("dp", "tensor"),
            P("dp", "tensor"),
            P("dp", "tensor"),
            P("dp", "tensor"),
            P(),
            P("dp", "tensor"),
            P("dp", "tensor"),
            P("dp", "tensor"),
            P("dp", "tensor"),
            P("dp", "tensor"),
            P("dp", "tensor"),
            P("dp", "tensor"),
            P(None, "dp"),
            P("dp", "tensor"),
            P("dp", "tensor"),
            P("dp", "tensor"),
            P("dp", "tensor"),
            P("dp", "tensor"),
            P("dp", "tensor"),
            P("dp", "tensor"),
            P(None, "dp"),
        ),
        out_specs=(
            P("dp", None),
            P("dp", None),
            P(),
            P("dp", "tensor"),
            P("dp", "tensor"),
            P("dp", "tensor"),
            P("dp", "tensor"),
            P("dp", "tensor"),
            P("dp", "tensor"),
            P("dp", "tensor"),
            P(None, "dp"),
            P("dp", "tensor"),
            P("dp", "tensor"),
            P("dp", "tensor"),
            P("dp", "tensor"),
            P("dp", "tensor"),
            P("dp", "tensor"),
            P("dp", "tensor"),
            P(None, "dp"),
            P("dp", "tensor"),
            P("dp", "tensor"),
            P("dp", "tensor"),
            P("dp", "tensor"),
            P("dp", "tensor"),
            P("dp", "tensor"),
            P("dp", "tensor"),
            P(None, "dp"),
        ),
        check_vma=False,
    )
```

time: 960 us -> 622 us (0.65)
  matrix products: 130 us -> 0 us
  Pallas kernels: 681 us -> 576 us
  other arithmetic: 110 us -> 27 us
  waiting for transfers between devices: 9.77 us -> 0 us
    dot_general x9 -> x0, matrix products: 130 us -> none  [product(): lax.dot_general(left, right, (((left_dim,), (right_dim,)), ((), ())), pre...]
    pallas_call x10 -> x2, Pallas kernels: 681 us -> 576 us  [chain(): pl.pallas_call(kernel, name=name, in_specs=[ANYWHERE] * len(arrays) + [sp...]
    reduce_sum x10 -> x1, other arithmetic: 38.9 us -> 1.24 us  [local(): jnp.sum(made[Name.square_sum]) + jnp.sum(jnp.square(gain_sum))]
    add x2 -> x1, other arithmetic: 35.8 us -> 11.6 us  [local(): in_grad = made[Name.dmiddle].astype(F32) + made[Name.change].astype(F32)]
    convert_element_type x5 -> x0, other arithmetic: 15.7 us -> none  [the longest x1 8.32 us: local(): normed_two = (middle * inverse_two * norm_gains[1]).astype(BF16)]
    ppermute x4 -> x0, waiting for transfers between devices: 9.77 us -> none  [tensor_sum(): other = lax.ppermute(partial, 'tensor', [(0, 1), (1, 0)])]
  transfers between devices with their start and end apart: 4 -> 0, of which waited for: 1 -> 0; matrix products, arithmetic and copies ran while one was open for 12% -> 0% of each run, Pallas kernels for 23% -> 0%
where the time goes in v2:
time: 622 us; the launch traced here: 611 us
  Pallas kernels  576 us (93%)
  other arithmetic  27 us (4%)
    pallas_call x2, Pallas kernels, chain(): pl.pallas_call(kernel, name=name, in_specs=[ANYWHERE] * len(arrays) + [sp...  576 us

profile of v2, /device:TPU:0, one launch (start us, length us, event | category | flops | bytes accessed | tf_op | source)
XLA Modules:
  0.0 610.8 jit_solution(2726230978738680217)
XLA Ops:
  0.7 1.5 fusion.5
  2.2 240.4 %forward.1 = (bf16[2048,1536]{1,0:T(8,128)(2,1)}, bf16[1536,2048]{1,0:T(8,128)(2,1)}, bf16[768,2048]{1,0:T(8,128)(2,1)}, f32[4,2,2048]{2,1,0:T(2,128)}, bf16[204...) custom-call(bf16[2048,1536]{1,0:T(8,128)(2,1)} %everything_1_.1, ...), custom_call_target="tpu_custom_call" | custom-call | tf_op jit(solution)/shard_map/forward/pallas_call | solution.py:663
  242.6 0.0 copy-start.20
  242.6 0.0 copy-start.21
  242.7 0.0 copy-start
  242.7 0.0 copy-start.1
  242.7 335.8 %backward.1 = (bf16[2048,2048]{1,0:T(8,128)(2,1)}, bf16[2048,2048]{1,0:T(8,128)(2,1)}, bf16[4,2,2,96,2048]{4,3,2,1,0:T(8,128)(2,1)}, bf16[4,2,2,96,2048]{4,3,2,1...) custom-call(bf16[2048,1536]{1,0:T(8,128)(2,1)} %everything_0_.3, ...), custom_call_target="tpu_custom_call" | custom-call | tf_op jit(solution)/shard_map/backward/pallas_call | solution.py:663
  578.5 0.0 copy-start.2
  578.5 1.4 multiply_reduce_fusion
  579.9 1.2 reduce_sum.18
  582.5 0.0 copy-start.5
  582.5 0.0 copy-start.6
  582.5 0.0 copy-start.7
  583.4 0.0 copy-done.20
  583.4 0.0 copy-done.21
  583.4 1.4 add_subtract_fusion.1
  584.8 0.0 copy-done
  584.8 0.0 copy-done.1
  584.8 0.0 copy-start.9
  584.8 0.0 copy-start.10
  584.8 0.0 copy-start.16
  584.8 0.0 copy-start.17
  584.9 0.0 copy-start.18
  584.9 0.0 copy-start.19
  584.9 5.4 multiply_subtract_fusion
  590.3 0.0 copy-start.12
  590.3 0.0 copy-start.13
  590.4 0.0 copy-start.14
  590.4 0.0 copy-start.15
  590.4 0.0 copy-done.2
  590.4 0.0 copy-done.5
  590.4 0.0 copy-done.6
  590.4 0.0 copy-done.7
  590.4 1.9 multiply_subtract_fusion.2
  592.3 0.0 copy-done.8
  592.3 0.0 copy-done.9
  592.3 0.0 copy-done.10
  592.3 0.0 copy-done.16
  592.3 1.0 multiply_subtract_fusion.4
  593.4 0.0 copy-done.11
  593.4 0.0 copy-done.12
  593.4 0.0 copy-done.13
  593.4 0.0 copy-done.14
  593.4 0.0 copy-done.15
  593.4 0.0 slice-start
  593.4 1.5 add_subtract_fusion
  594.9 11.6 %convert_add_fusion = f32[2048,1536]{1,0:T(8,128)} fusion(bf16[2048,1536]{1,0:T(8,128)(2,1)} %get-tuple-element.69, bf16[2048,1536]{1,0:T(8,128)(2,1)} %get-tuple-element.68), kind=kLoop, calls=%fused_computation | loop fusion | flops 9437184 | bytes 25165824 | tf_op jit(solution)/shard_map/add | solution.py:1360
  606.6 2.7 copy.57
  (14 shorter events, 0.0 us)
Async XLA Ops:
  242.6 340.8 %copy-start.20 = (f32[2,96]{1,0:T(2,128)S(1)}, f32[2,96]{1,0:T(2,128)}, u32[]{:S(2)}) copy-start(f32[2,96]{1,0:T(2,128)} %param.55) | copy-start | bytes 2308
  242.6 340.8 %copy-start.21 = (f32[2,96]{1,0:T(2,128)S(1)}, f32[2,96]{1,0:T(2,128)}, u32[]{:S(2)}) copy-start(f32[2,96]{1,0:T(2,128)} %param.47) | copy-start | bytes 2308
  242.7 342.1 %copy-start = (f32[96,2048]{1,0:T(8,128)S(1)}, f32[96,2048]{1,0:T(8,128)}, u32[]{:S(2)}) copy-start(f32[96,2048]{1,0:T(8,128)} %everything_11_.1) | copy-start | bytes 2359300
  242.7 342.1 %copy-start.1 = (f32[96,2048]{1,0:T(8,128)S(1)}, f32[96,2048]{1,0:T(8,128)}, u32[]{:S(2)}) copy-start(f32[96,2048]{1,0:T(8,128)} %everything_12_.1) | copy-start | bytes 2359300
  578.5 11.9 %copy-start.2 = (f32[96,2048]{1,0:T(8,128)S(1)}, f32[96,2048]{1,0:T(8,128)}, u32[]{:S(2)}) copy-start(f32[96,2048]{1,0:T(8,128)} %everything_10_.1) | copy-start | bytes 2359300
  582.5 7.9 %copy-start.5 = (f32[96,2048]{1,0:T(8,128)S(1)}, f32[96,2048]{1,0:T(8,128)}, u32[]{:S(2)}) copy-start(f32[96,2048]{1,0:T(8,128)} %param.52) | copy-start | bytes 2359300
  582.5 7.9 %copy-start.6 = (f32[96,2048]{1,0:T(8,128)S(1)}, f32[96,2048]{1,0:T(8,128)}, u32[]{:S(2)}) copy-start(f32[96,2048]{1,0:T(8,128)} %param.44) | copy-start | bytes 2359300
  582.5 7.9 %copy-start.7 = (f32[96,2048]{1,0:T(8,128)S(1)}, f32[96,2048]{1,0:T(8,128)}, u32[]{:S(2)}) copy-start(f32[96,2048]{1,0:T(8,128)} %get-tuple-element.74) | copy-start | bytes 2359300
  584.8 7.5 %copy-start.8 = (f32[96,384]{1,0:T(8,128)S(1)}, f32[96,384]{1,0:T(8,128)}, u32[]{:S(2)}) copy-start(f32[96,384]{1,0:T(8,128)} %everything_7_.1) | copy-start | bytes 442372
  584.8 7.5 %copy-start.9 = (f32[96,384]{1,0:T(8,128)S(1)}, f32[96,384]{1,0:T(8,128)}, u32[]{:S(2)}) copy-start(f32[96,384]{1,0:T(8,128)} %everything_8_.1) | copy-start | bytes 442372
  584.8 7.5 %copy-start.10 = (f32[96,1536]{1,0:T(8,128)S(1)}, f32[96,1536]{1,0:T(8,128)}, u32[]{:S(2)}) copy-start(f32[96,1536]{1,0:T(8,128)} %get-tuple-element.72) | copy-start | bytes 1769476
  584.8 7.5 %copy-start.16 = (f32[96,384]{1,0:T(8,128)S(1)}, f32[96,384]{1,0:T(8,128)}, u32[]{:S(2)}) copy-start(f32[96,384]{1,0:T(8,128)} %param.50) | copy-start | bytes 442372
  584.8 7.5 %copy-start.17 = (f32[96,384]{1,0:T(8,128)S(1)}, f32[96,384]{1,0:T(8,128)}, u32[]{:S(2)}) copy-start(f32[96,384]{1,0:T(8,128)} %param.42) | copy-start | bytes 442372
  584.9 7.5 %copy-start.18 = (f32[96,384]{1,0:T(8,128)S(1)}, f32[96,384]{1,0:T(8,128)}, u32[]{:S(2)}) copy-start(f32[96,384]{1,0:T(8,128)} %param.49) | copy-start | bytes 442372
  584.9 7.5 %copy-start.19 = (f32[96,384]{1,0:T(8,128)S(1)}, f32[96,384]{1,0:T(8,128)}, u32[]{:S(2)}) copy-start(f32[96,384]{1,0:T(8,128)} %param.41) | copy-start | bytes 442372
  590.3 3.1 copy-start.3
  590.3 3.1 copy-start.4
  590.3 3.1 copy-start.11
  590.3 3.1 copy-start.12
  590.3 3.1 copy-start.13
  590.4 3.1 copy-start.14
  590.4 3.1 copy-start.15
  593.4 13.1 %slice-start = ((s8[6291456]{0:T(1024)(128)(4,1)}), s8[4194304]{0:T(1024)(128)(4,1)S(1)}, s32[]{:S(2)}) async-start(s8[6291456]{0:T(1024)(128)(4,1)} %bitcast.11), calls=%async_computation | async-start | bytes 8388608
  594.9 11.6 %slice-start.1 = ((s8[6291456]{0:T(1024)(128)(4,1)}), s8[2097152]{0:T(1024)(128)(4,1)S(1)}, s32[]{:S(2)}) async-start(s8[6291456]{0:T(1024)(128)(4,1)} %bitcast.11), calls=%async_computation.1 | async-start | bytes 4194304

commit v3 on v2

--- a/solution.py
+++ b/solution.py
@@ -40,7 +40,7 @@
 class Name(enum.Enum):
     block_in = enum.auto()
     block_out = enum.auto()
-    change = enum.auto()
+    in_grad = enum.auto()
     cosine = enum.auto()
     dgate = enum.auto()
     dmiddle = enum.auto()
@@ -263,6 +263,18 @@
             view(self.grad, {first: self.place.at[first]}, self.columns), self.mine, self.local
         )
 
+    def add(self, target, value, landing, stage):
+        slots = self.place.dims[self.order[stage]] - 1
+        if slots == 1:
+            target[...] = value + landing[0]
+        elif slots > 1:
+            value = value.astype(F32)
+            for slot in range(slots):
+                value = value + landing[slot].astype(F32)
+            target[...] = value.astype(BF16)
+        else:
+            target[...] = value
+
     def act(self, phase):
         place, order = self.place, self.order
         if phase == 0:
@@ -272,28 +284,10 @@
                 copy.wait_recv()
         if phase == 1:
             self.own().wait()
-            outer, inner = (place.dims[d] for d in self.rest)
-
-            def add_first(item, carry):
-                i, j = item // inner, lax.rem(item, inner)
-                value = self.mine[i, j].astype(F32)
-                for slot in range(place.dims[order[0]] - 1):
-                    value = value + self.landings[0][slot, i, j].astype(F32)
-                self.total[i, j] = value.astype(BF16)
-                return carry
-
-            lax.fori_loop(0, outer * inner, add_first, 0)
+            self.add(self.total, self.mine[...], self.landings[0], 0)
         if phase == 2:
-
-            def add_second(item, carry):
-                spot = self.pick(place.at[order[1]], item)
-                value = self.total[spot].astype(F32)
-                for slot in range(place.dims[order[1]] - 1):
-                    value = value + self.landings[1][slot, item].astype(F32)
-                self.total[spot] = value.astype(BF16)
-                return carry
-
-            lax.fori_loop(0, place.dims[order[2]], add_second, 0)
+            spot = self.total.at[self.pick(place.at[order[1]], slice(None))]
+            self.add(spot, spot[...], self.landings[1], 1)
         if phase < 3:
             for copy in self.copies(phase, False):
                 copy.start()
@@ -318,6 +312,17 @@
     return first, second
 
 
+def woven(plan, pair):
+    first, second = ([c for c in side if c[0] not in pair] for side in plan)
+    count = sum(len(side) for side in plan) - len(first) - len(second)
+    later = [3, 5, 7] if count == 16 else list(range(count // 2 - 1, 0, -3))
+    chunks = [(which, (i * CHUNK, CHUNK)) for i in range(count // 2) for which in pair]
+    for side, keep in ((first, False), (second, True)):
+        at = sum(1 for which, _ in side if which < pair[0])
+        side[at:at] = [c for c in chunks if (c[1][0] // CHUNK in later) == keep]
+    return first, second
+
+
 def slots_of(first, second, stride=2):
     rows = []
     for slot in range(max(first, second) + 3 * stride):
@@ -333,13 +338,13 @@
 
 
 class Gather:
-    def __init__(self, shards, dims):
+    def __init__(self, shards, dims, pair):
         self.dims, self.names = dims, list(shards)
         self.parts = [[part.shape[1] for part in parts] for parts in shards.values()]
         self.operands = [part for parts in shards.values() for part in parts]
         self.widths = [sum(widths) for widths in self.parts]
         self.rows = self.operands[0].shape[0]
-        self.plan = chunks_of(self.widths)
+        self.plan = woven(chunks_of(self.widths), pair)
         self.count = sum(len(p) for p in self.plan)
         self.slots = slots_of(*(len(p) for p in self.plan))
         self.in_specs = [ANYWHERE] * len(self.operands)
@@ -472,11 +477,12 @@
     return len(plan.slots)
 
 
-def done_row(plan, which):
+def done_row(plan, which, end=None):
     last = 0
     for number, row in enumerate(plan.slots):
         for order, chunk, phase in row:
-            if phase == 3 and plan.plan[order][chunk][0] in which:
+            array, (column, _) = plan.plan[order][chunk]
+            if phase == 3 and array in which and (end is None or column < end):
                 last = number + 1
     return last
 
@@ -494,8 +500,10 @@
         until=0,
         enter=None,
         after=None,
+        marks=None,
     ):
         self.body, self.grid, self.enter, self.after = body, grid, enter, after
+        self.marks = marks
         self.in_specs, self.out_specs = in_specs, out_specs
         self.inputs, self.outputs = inputs, outputs
         self.before, self.until = before, until
@@ -634,12 +642,17 @@
                 phase.enter(refs)
             steps = math.prod(phase.grid)
             marks = [done + (until - done) * number // steps for number in range(steps + 1)]
+            if phase.marks is not None:
+                marks = [done, *(max(done, mark) for mark in phase.marks)]
+                until = marks[-1]
 
             def body(*blocks, phase=phase, marks=marks, steps=steps):
                 index = tuple(pl.program_id(axis) for axis in range(len(phase.grid)))
                 step = 0
                 for position, extent in zip(index, phase.grid):
                     step = step * extent + position
+                if phase.marks is not None:
+                    phase.body(refs, index, *blocks)
                 for number in range(steps):
                     if marks[number] < marks[number + 1]:
 
@@ -647,7 +660,8 @@
                         def _(number=number):
                             run(marks[number], marks[number + 1])
 
-                phase.body(refs, index, *blocks)
+                if phase.marks is None:
+                    phase.body(refs, index, *blocks)
 
             pltpu.emit_pipeline(
                 body, grid=phase.grid, in_specs=phase.in_specs, out_specs=phase.out_specs
@@ -921,12 +935,12 @@
         up_ref[...] = up.astype(BF16)
         hidden_ref[...] = (gate * jax.nn.sigmoid(gate) * up).astype(BF16)
 
-    weight = pl.BlockSpec(lead + (wide,), lambda i, j: (0, 0, 0, 0, j))
-    out = pl.BlockSpec((tall, wide), lambda i, j: (i, j))
+    weight = pl.BlockSpec(lead + (wide,), lambda j, i: (0, 0, 0, 0, j))
+    out = pl.BlockSpec((tall, wide), lambda j, i: (i, j))
     return Phase(
         body,
-        (tokens // tall, units // wide),
-        [pl.BlockSpec((tall, width), lambda i, j: (i, 0)), weight, weight],
+        (units // wide, tokens // tall),
+        [pl.BlockSpec((tall, width), lambda j, i: (i, 0)), weight, weight],
         [out, out, out],
         [Name.normed_two, Name.gate_full, Name.up_full],
         [Name.gate, Name.up, Name.hidden],
@@ -935,7 +949,7 @@
 
 
 def feed_backward_phase(tokens, width, units, **timing):
-    tall, wide = 512, 512
+    tall, wide = 1024, 256
 
     def body(refs, index, d_ref, down_w, gate_ref, up_ref, dgate_ref, dup_ref):
         dhidden = product(d_ref[...], down_w[...])
@@ -1024,20 +1038,28 @@
     total[row : row + 1] += jnp.sum(value, 0, keepdims=True)
 
 
-def norm_back_phase(tokens, width, row, inputs, output, add, **timing):
-    def body(refs, index, row_ref, back_ref, out_ref):
+def norm_back_phase(tokens, width, row, inputs, outputs, features=None, **timing):
+    def body(refs, index, row_ref, back_ref, *others):
         dnorm = received(refs, index[0], tokens, width, PARTIAL_COLUMNS)
         values = row_ref[...].astype(F32)
         inverse = row_scale(values)
         unit = values * inverse
         add_gain(refs, row, index[0], dnorm * unit)
         change = norm_back(dnorm, refs[Name.gains][row : row + 1], unit, inverse)
-        if add:
-            change = change + back_ref[...].astype(F32)
-        out_ref[...] = change.astype(BF16)
+        total = (back_ref[...].astype(F32) + change).astype(BF16)
+        if features is None:
+            others[0][...] = total
+        else:
+            w_ref, out_ref, mixed_ref = others
+            out_ref[...] = total
+            mixed_ref[...] = product(w_ref[...], total, 0, 1).astype(BF16)
 
     rows = row_blocks(width)
-    return Phase(body, (tokens // 256,), [rows, rows], [rows], inputs, [output], **timing)
+    in_specs, out_specs = [rows, rows], [rows]
+    if features is not None:
+        in_specs.append(whole((width, features)))
+        out_specs.append(pl.BlockSpec((features, 256), lambda i: (0, i)))
+    return Phase(body, (tokens // 256,), in_specs, out_specs, inputs, outputs, **timing)
 
 
 def block_out_phase(tokens, width, **timing):
@@ -1048,23 +1070,6 @@
     rows = row_blocks(width)
     return Phase(
         body, (tokens // 256,), [rows], [rows], [Name.middle], [Name.block_out], **timing
-    )
-
-
-def mixed_grad_phase(tokens, width, features, **timing):
-    block = 512
-
-    def body(refs, index, w_ref, d_ref, out_ref):
-        out_ref[...] = product(w_ref[...], d_ref[...], 0, 1).astype(BF16)
-
-    return Phase(
-        body,
-        (tokens // block,),
-        [whole((width, features)), pl.BlockSpec((block, width), lambda i: (i, 0))],
-        [pl.BlockSpec((features, block), lambda i: (0, i))],
-        [Name.o_full, Name.dmiddle],
-        [Name.dmixed],
-        **timing,
     )
 
 
@@ -1136,22 +1141,29 @@
             Name.down_full: [down_weight],
         },
         dims,
+        (2, 3),
     )
     first = done_row(plan, (0,))
     then = done_row(plan, (1,))
-    later = done_row(plan, (2, 3))
+    starts = [done_row(plan, (2, 3), end) for end in range(512, units + 1, 512)]
+    soon = starts[0]
+    held = [mark for mark in [*starts[1:], starts[-1]] for _ in range(tokens // 1024)]
+    held = [
+        max(mark, len(plan.slots) - 2 - (len(held) - number) * 5 // len(held))
+        for number, mark in enumerate(held, 1)
+    ]
     made = chain(
         "forward",
         [
             project_phase(
-                tokens, width, features, lead + (features,), before=first, until=first + 2
+                tokens, width, features, lead + (features,), before=first, until=first + 3
             ),
             attend_forward_phase(tokens, features, until=max(then, first + 8)),
             attention_out_phase(
-                tokens, width, lead + (q_width,), before=then, until=(first + 8 + later) // 2
+                tokens, width, lead + (q_width,), before=then, until=max(then, first + 10)
             ),
-            second_norm_phase(tokens, width, until=later),
-            feed_forward_phase(tokens, lead, units, before=later, until=len(plan.slots) - 2),
+            second_norm_phase(tokens, width, until=max(soon, first + 11)),
+            feed_forward_phase(tokens, lead, units, before=soon, marks=held),
             weight_grad_phase(
                 tokens,
                 lead,
@@ -1275,13 +1287,12 @@
                 tokens,
                 width,
                 1,
-                [Name.middle, Name.out_grad],
-                Name.dmiddle,
-                True,
-                until=gate_row + 7,
+                [Name.middle, Name.out_grad, Name.o_full],
+                [Name.dmiddle, Name.dmixed],
+                q_width,
+                until=gate_row + 8,
                 after=Exchange.release,
             ),
-            mixed_grad_phase(tokens, width, q_width, until=gate_row + 8),
             weight_grad_phase(
                 tokens,
                 lead,
@@ -1308,8 +1319,7 @@
                 width,
                 0,
                 [Name.block_in, Name.dmiddle],
-                Name.change,
-                False,
+                [Name.in_grad],
                 until=qkv_row + 4,
                 after=share_gains,
             ),
@@ -1340,7 +1350,7 @@
             Name.grad_out: out_like(*lead, q_width),
             Name.dqkv: out_like(features, tokens),
             Name.grad_qkv: out_like(*lead, features),
-            Name.change: per_token,
+            Name.in_grad: per_token,
             Name.block_out: per_token,
         },
         {
@@ -1357,7 +1367,7 @@
         for name in (Name.sum_qkv, Name.sum_out, Name.sum_gate, Name.sum_up, Name.sum_down)
     )
     block_out = made[Name.block_out]
-    in_grad = made[Name.dmiddle].astype(F32) + made[Name.change].astype(F32)
+    in_grad = made[Name.in_grad].astype(F32)
     gain_sum = made[Name.gain_sum]
     total_square = jnp.sum(made[Name.square_sum]) + jnp.sum(jnp.square(gain_sum))
     gain_width = width // devices

time: 622 us -> 605 us (0.973)
  Pallas kernels: 576 us -> 564 us
    pallas_call x2, Pallas kernels: 576 us -> 564 us  [chain(): pl.pallas_call(kernel, name=name, in_specs=[ANYWHERE] * len(arrays) + [sp...]
    add x1 -> x0, other arithmetic: 11.6 us -> none  [local(): in_grad = made[Name.dmiddle].astype(F32) + made[Name.change].astype(F32)]
    convert_element_type x0 -> x1, other arithmetic: none -> 6.56 us  [local(): in_grad = made[Name.in_grad].astype(F32)]
where the time goes in v3:
time: 605 us; the launch traced here: 594 us
  Pallas kernels  564 us (93%)
  other arithmetic  21.9 us (4%)
    pallas_call x2, Pallas kernels, chain(): pl.pallas_call(kernel, name=name, in_specs=[ANYWHERE] * len(arrays) + [sp...  564 us

profile of v3, /device:TPU:0, one launch (start us, length us, event | category | flops | bytes accessed | tf_op | source)
XLA Modules:
  0.0 593.6 jit_solution(6978921659968447978)
XLA Ops:
  0.7 1.5 fusion.5
  2.2 238.9 %forward.1 = (bf16[2048,1536]{1,0:T(8,128)(2,1)}, bf16[1536,2048]{1,0:T(8,128)(2,1)}, bf16[768,2048]{1,0:T(8,128)(2,1)}, f32[4,2,2048]{2,1,0:T(2,128)}, bf16[204...) custom-call(bf16[2048,1536]{1,0:T(8,128)(2,1)} %everything_1_.1, ...), custom_call_target="tpu_custom_call" | custom-call | tf_op jit(solution)/shard_map/forward/pallas_call | solution.py:677
  241.1 0.0 copy-start.20
  241.1 0.0 copy-start.21
  241.1 0.0 copy-start
  241.1 0.0 copy-start.1
  241.2 325.2 %backward.1 = (bf16[2048,2048]{1,0:T(8,128)(2,1)}, bf16[2048,2048]{1,0:T(8,128)(2,1)}, bf16[4,2,2,96,2048]{4,3,2,1,0:T(8,128)(2,1)}, bf16[4,2,2,96,2048]{4,3,2,1...) custom-call(bf16[2048,1536]{1,0:T(8,128)(2,1)} %everything_0_.3, ...), custom_call_target="tpu_custom_call" | custom-call | tf_op jit(solution)/shard_map/backward/pallas_call | solution.py:677
  566.4 0.0 copy-start.2
  566.4 1.4 multiply_reduce_fusion
  567.8 1.2 reduce_sum.18
  570.4 0.0 copy-start.5
  570.4 0.0 copy-start.6
  570.4 0.0 copy-start.7
  571.3 0.0 copy-done.20
  571.3 0.0 copy-done.21
  571.3 1.4 add_subtract_fusion.1
  572.7 0.0 copy-done
  572.7 0.0 copy-done.1
  572.7 0.0 copy-start.9
  572.7 0.0 copy-start.10
  572.7 0.0 copy-start.16
  572.7 0.0 copy-start.17
  572.7 0.0 copy-start.18
  572.7 0.0 copy-start.19
  572.8 0.0 slice-start.2
  572.8 5.5 multiply_subtract_fusion
  578.3 0.0 copy-start.12
  578.3 0.0 copy-start.13
  578.3 0.0 copy-start.14
  578.3 0.0 copy-start.15
  578.3 0.0 copy-done.2
  578.3 0.0 copy-done.5
  578.3 0.0 copy-done.6
  578.3 0.0 copy-done.7
  578.3 0.0 slice-start.3
  578.4 1.8 multiply_subtract_fusion.2
  580.2 0.0 copy-done.8
  580.2 0.0 copy-done.9
  580.2 0.0 copy-done.10
  580.2 0.0 copy-done.16
  580.2 0.0 copy-done.17
  580.2 1.0 multiply_subtract_fusion.4
  581.3 0.0 copy-done.4
  581.3 0.0 slice-start
  581.3 1.5 add_subtract_fusion
  582.8 0.0 slice-done.2
  582.8 6.6 %convert_element_type.7 = f32[2048,1536]{1,0:T(8,128)} convert(bf16[2048,1536]{1,0:T(8,128)(2,1)S(1)} %bitcast.14) | non-fusion elementwise | flops 3145728 | bytes 18874368 | tf_op jit(solution)/shard_map/convert_element_type | solution.py:1370
  589.4 2.7 copy.57
  (19 shorter events, 0.0 us)
Async XLA Ops:
  241.1 330.2 %copy-start.20 = (f32[2,96]{1,0:T(2,128)S(1)}, f32[2,96]{1,0:T(2,128)}, u32[]{:S(2)}) copy-start(f32[2,96]{1,0:T(2,128)} %param.55) | copy-start | bytes 2308
  241.1 330.2 %copy-start.21 = (f32[2,96]{1,0:T(2,128)S(1)}, f32[2,96]{1,0:T(2,128)}, u32[]{:S(2)}) copy-start(f32[2,96]{1,0:T(2,128)} %param.47) | copy-start | bytes 2308
  241.1 331.5 %copy-start = (f32[96,2048]{1,0:T(8,128)S(1)}, f32[96,2048]{1,0:T(8,128)}, u32[]{:S(2)}) copy-start(f32[96,2048]{1,0:T(8,128)} %everything_11_.1) | copy-start | bytes 2359300
  241.1 331.5 %copy-start.1 = (f32[96,2048]{1,0:T(8,128)S(1)}, f32[96,2048]{1,0:T(8,128)}, u32[]{:S(2)}) copy-start(f32[96,2048]{1,0:T(8,128)} %everything_12_.1) | copy-start | bytes 2359300
  566.4 11.9 %copy-start.2 = (f32[96,2048]{1,0:T(8,128)S(1)}, f32[96,2048]{1,0:T(8,128)}, u32[]{:S(2)}) copy-start(f32[96,2048]{1,0:T(8,128)} %everything_10_.1) | copy-start | bytes 2359300
  570.4 7.9 %copy-start.5 = (f32[96,2048]{1,0:T(8,128)S(1)}, f32[96,2048]{1,0:T(8,128)}, u32[]{:S(2)}) copy-start(f32[96,2048]{1,0:T(8,128)} %param.52) | copy-start | bytes 2359300
  570.4 7.9 %copy-start.6 = (f32[96,2048]{1,0:T(8,128)S(1)}, f32[96,2048]{1,0:T(8,128)}, u32[]{:S(2)}) copy-start(f32[96,2048]{1,0:T(8,128)} %param.44) | copy-start | bytes 2359300
  570.4 7.9 %copy-start.7 = (f32[96,2048]{1,0:T(8,128)S(1)}, f32[96,2048]{1,0:T(8,128)}, u32[]{:S(2)}) copy-start(f32[96,2048]{1,0:T(8,128)} %get-tuple-element.72) | copy-start | bytes 2359300
  572.7 7.5 %copy-start.8 = (f32[96,384]{1,0:T(8,128)S(1)}, f32[96,384]{1,0:T(8,128)}, u32[]{:S(2)}) copy-start(f32[96,384]{1,0:T(8,128)} %everything_7_.1) | copy-start | bytes 442372
  572.7 7.5 %copy-start.9 = (f32[96,384]{1,0:T(8,128)S(1)}, f32[96,384]{1,0:T(8,128)}, u32[]{:S(2)}) copy-start(f32[96,384]{1,0:T(8,128)} %everything_8_.1) | copy-start | bytes 442372
  572.7 7.5 %copy-start.10 = (f32[96,1536]{1,0:T(8,128)S(1)}, f32[96,1536]{1,0:T(8,128)}, u32[]{:S(2)}) copy-start(f32[96,1536]{1,0:T(8,128)} %get-tuple-element.70) | copy-start | bytes 1769476
  572.7 7.5 %copy-start.16 = (f32[96,384]{1,0:T(8,128)S(1)}, f32[96,384]{1,0:T(8,128)}, u32[]{:S(2)}) copy-start(f32[96,384]{1,0:T(8,128)} %param.50) | copy-start | bytes 442372
  572.7 7.5 %copy-start.17 = (f32[96,384]{1,0:T(8,128)S(1)}, f32[96,384]{1,0:T(8,128)}, u32[]{:S(2)}) copy-start(f32[96,384]{1,0:T(8,128)} %param.42) | copy-start | bytes 442372
  572.7 7.5 %copy-start.18 = (f32[96,384]{1,0:T(8,128)S(1)}, f32[96,384]{1,0:T(8,128)}, u32[]{:S(2)}) copy-start(f32[96,384]{1,0:T(8,128)} %param.49) | copy-start | bytes 442372
  572.7 7.5 %copy-start.19 = (f32[96,384]{1,0:T(8,128)S(1)}, f32[96,384]{1,0:T(8,128)}, u32[]{:S(2)}) copy-start(f32[96,384]{1,0:T(8,128)} %param.41) | copy-start | bytes 442372
  572.8 10.0 %slice-start.2 = ((s8[6291456]{0:T(1024)(128)(4,1)}), s8[4194304]{0:T(1024)(128)(4,1)S(1)}, s32[]{:S(2)}) async-start(s8[6291456]{0:T(1024)(128)(4,1)} %bitcast.13), calls=%async_computation.2 | async-start | bytes 8388608
  578.2 3.0 copy-start.3
  578.2 3.0 copy-start.4
  578.3 3.0 copy-start.11
  578.3 3.0 copy-start.12
  578.3 3.0 copy-start.13
  578.3 3.0 copy-start.14
  578.3 3.0 copy-start.15
  578.3 4.5 slice-start.3
  581.3 8.1 %slice-start = ((s8[6291456]{0:T(1024)(128)(4,1)}), s8[4194304]{0:T(1024)(128)(4,1)S(1)}, s32[]{:S(2)}) async-start(s8[6291456]{0:T(1024)(128)(4,1)} %bitcast.11), calls=%async_computation | async-start | bytes 8388608
  582.8 6.6 %slice-start.1 = ((s8[6291456]{0:T(1024)(128)(4,1)}), s8[2097152]{0:T(1024)(128)(4,1)S(1)}, s32[]{:S(2)}) async-start(s8[6291456]{0:T(1024)(128)(4,1)} %bitcast.11), calls=%async_computation.1 | async-start | bytes 4194304
